TPU v7x, 256 devices: a whole 4x4x8 slice. The times are simulated.
256 devices in a mesh: heads: 8 (over x, y_lo), tok: 32 (over z, y_hi, core).
Axes of the slice: x: 4, y: 4 (y_hi: 2, y_lo: 2; y = y_hi * 2 + y_lo), z: 8, core: 2. Of those that a mesh axis runs over, the one named last changes fastest.
Arguments:
- queries: bfloat16 [32, 16, 32, 1024], P('tok', None, None, 'heads'), may hold values from -12 to 12
- key_rows: bfloat16 [32, 16, 32, 1024], P('tok', None, None, 'heads'), may hold values from -6 to 6
- value_rows: bfloat16 [32, 16, 32, 1024], P('tok', None, None, 'heads'), may hold values from -6 to 6
- residual: bfloat16 [16, 32, 32, 1024], P('heads', 'tok'), may hold values from -3 to 3
- w_out: bfloat16 [1024, 1024], P('heads'), may hold values from -0.375 to 0.375
- w_neck: bfloat16 [1024, 256], replicated, may hold values from -0.1875 to 0.1875
- w_first: bfloat16 [3, 3, 3, 256, 256], replicated, may hold values from -0.109375 to 0.109375
- w_second: bfloat16 [3, 3, 3, 256, 256], replicated, may hold values from -0.109375 to 0.109375
- w_class: bfloat16 [256], replicated, may hold values from -0.5 to 0.5
- labels: int32 [16, 32, 32], P('heads', None, 'tok'), may hold values from 0 to 1, as said below
Outputs:
- encoded: bfloat16 [16, 32, 32, 1024], P('heads', 'tok')
- dice_loss: float32 [], replicated
- grad_encoded: bfloat16 [16, 32, 32, 1024], P('heads', 'tok')
Inputs may be any that keep to these rules, and one draw needn't show every extreme that they name: `labels`: 1 marks a fault cell.
All inputs are finite; a program needn't handle non-finite values.
Results may differ from a plain program's by a relative error of at most 0.025.
Values may be sent and summed in bfloat16 or wider, within the bound.
A program may use at most 128 MiB of HBM per device.

v0:
```python
import jax
import jax.numpy as jnp
from jax import lax
from jax.sharding import PartitionSpec as P

HD = 64


OFFSETS = [
    (along_c, along_t, along_x)
    for along_c in range(3)
    for along_t in range(3)
    for along_x in range(3)
]
LOSS_SCALE = 64.0
NEG_LARGE = -1e30


def padded_2(value, sides, width):
    for axis, dim in sides:
        size, length = (lax.axis_size(axis), value.shape[dim])
        up = [(i, (i + 1) % size) for i in range(size - 1)]
        down = [(j, i) for i, j in up]
        last = lax.slice_in_dim(value, length - width, length, axis=dim)
        first = lax.slice_in_dim(value, 0, width, axis=dim)
        before = lax.ppermute(last, axis, up)
        after = lax.ppermute(first, axis, down)
        value = jnp.concatenate([before, value, after], axis=dim)
    return value


def silu_slope(volume):
    sigma = jax.nn.sigmoid(volume)
    return sigma * (1.0 + volume * (1.0 - sigma))


def with_rims(volume):
    padded = padded_2(volume, (("heads", 0), ("tok", 2)), 1)
    return jnp.pad(padded, ((0, 0), (1, 1), (0, 0), (0, 0)))


def conv_apply(volume, weights, flipped):
    extent = volume.shape[:3]
    padded = with_rims(volume)
    pieces = []
    for along_c, along_t, along_x in OFFSETS:
        if flipped:
            anchor = (2 - along_c, 2 - along_t, 2 - along_x)
        else:
            anchor = (along_c, along_t, along_x)
        pieces.append(
            padded[
                anchor[0] : anchor[0] + extent[0],
                anchor[1] : anchor[1] + extent[1],
                anchor[2] : anchor[2] + extent[2],
            ]
        )
    stacked = jnp.stack(pieces, axis=3)
    columns = stacked.reshape(extent[0] * extent[1] * extent[2], 27, volume.shape[3])
    kernel = weights.reshape(27, weights.shape[3], weights.shape[4])
    if flipped:
        contraction = (((1, 2), (0, 2)), ((), ()))
    else:
        contraction = (((1, 2), (0, 1)), ((), ()))
    return lax.dot_general(columns, kernel, contraction, preferred_element_type=jnp.float32)


def online_step(carried, query_block, key_block, value_block, scale):
    row_peak, totals, weighted_sum = carried
    scores = (
        jnp.einsum("qhd,khd->qhk", query_block, key_block, preferred_element_type=jnp.float32)
        * scale
    )
    new_peak = jnp.maximum(row_peak, jnp.max(scores, axis=-1))
    factor = jnp.exp(row_peak - new_peak)
    raw_weights = jnp.exp(scores - new_peak[:, :, None])
    totals = totals * factor + jnp.sum(raw_weights, axis=-1)
    weighted_sum = weighted_sum * factor[:, :, None] + jnp.einsum(
        "qhk,khd->qhd",
        raw_weights.astype(jnp.bfloat16),
        value_block,
        preferred_element_type=jnp.float32,
    )
    return (new_peak, totals, weighted_sum)


def on_device(
    queries, key_rows, value_rows, residual, w_out, w_neck, w_first, w_second, w_class, labels
):
    width_here = queries.shape[-1]
    heads_here = width_here // HD
    scale = HD ** (-0.5)
    local_queries = queries.reshape(-1, heads_here, HD)
    query_total = local_queries.shape[0]
    start_state = (
        jnp.full((query_total, heads_here), NEG_LARGE, jnp.float32),
        jnp.zeros((query_total, heads_here), jnp.float32),
        jnp.zeros((query_total, heads_here, HD), jnp.float32),
    )
    key_flat = lax.all_gather(key_rows, "tok", axis=0, tiled=True).reshape(-1, heads_here, HD)
    value_flat = lax.all_gather(value_rows, "tok", axis=0, tiled=True).reshape(-1, heads_here, HD)
    key_total = key_flat.shape[0]
    key_blocks = key_flat.reshape(key_total // 512, 512, heads_here, HD)
    value_blocks = value_flat.reshape(key_total // 512, 512, heads_here, HD)

    def scan_step(inner, paired):
        return (online_step(inner, local_queries, paired[0], paired[1], scale), None)

    row_peak, totals, weighted_sum = lax.scan(scan_step, start_state, (key_blocks, value_blocks))[0]
    attended = (weighted_sum / totals[:, :, None]).astype(jnp.bfloat16)
    attended_grid = attended.reshape(queries.shape)
    attention_out = lax.psum_scatter(
        jnp.einsum(
            "tzxe,ed->ztxd", attended_grid, w_out, preferred_element_type=jnp.float32
        ).astype(jnp.bfloat16),
        "heads",
        scatter_dimension=0,
        tiled=True,
    ).astype(jnp.float32)
    encoded = (residual.astype(jnp.float32) + attention_out).astype(jnp.bfloat16)
    tiled = lax.all_to_all(encoded, "tok", split_axis=2, concat_axis=1, tiled=True)
    neck_feats = jnp.einsum(
        "ztxd,dc->ztxc", tiled, w_neck, preferred_element_type=jnp.float32
    ).astype(jnp.bfloat16)
    extent = neck_feats.shape[:3]
    channels = w_neck.shape[1]
    cell_count = extent[0] * extent[1] * extent[2]
    hidden_one = conv_apply(neck_feats, w_first, False)
    active_one = jax.nn.silu(hidden_one).astype(jnp.bfloat16)
    hidden_two = conv_apply(active_one.reshape(extent + (channels,)), w_second, False)
    active_two = jax.nn.silu(hidden_two).astype(jnp.bfloat16)
    logits = jnp.dot(active_two, w_class, preferred_element_type=jnp.float32)
    probability = jax.nn.sigmoid(logits)
    fault_mask = labels.reshape(cell_count).astype(jnp.float32)
    intersection, total_prob, total_fault = lax.psum(
        (jnp.sum(probability * fault_mask), jnp.sum(probability), jnp.sum(fault_mask)),
        ("heads", "tok"),
    )
    dice_denominator = total_prob + total_fault
    dice_loss = 1.0 - 2.0 * intersection / dice_denominator
    cells_all = float(cell_count * lax.axis_size("heads") * lax.axis_size("tok"))
    grad_logits = (
        LOSS_SCALE
        * cells_all
        * -2.0
        * (fault_mask * dice_denominator - intersection)
        / (dice_denominator * dice_denominator)
        * probability
        * (1.0 - probability)
    )
    grad_hidden_two = (
        grad_logits[:, None] * w_class.astype(jnp.float32)[None, :] * silu_slope(hidden_two)
    ).astype(jnp.bfloat16)
    grad_active_one = conv_apply(grad_hidden_two.reshape(extent + (channels,)), w_second, True)
    grad_hidden_one = (grad_active_one * silu_slope(hidden_one)).astype(jnp.bfloat16)
    grad_neck = (
        conv_apply(grad_hidden_one.reshape(extent + (channels,)), w_first, True)
        .astype(jnp.bfloat16)
        .reshape(extent + (channels,))
    )
    grad_tiles = jnp.einsum(
        "ztxc,dc->ztxd", grad_neck, w_neck, preferred_element_type=jnp.float32
    ).astype(jnp.bfloat16)
    grad_encoded = lax.all_to_all(grad_tiles, "tok", split_axis=1, concat_axis=2, tiled=True)
    return (encoded, dice_loss, grad_encoded)


def solution(mesh):
    placed = (
        P("tok", None, None, "heads"),
        P("tok", None, None, "heads"),
        P("tok", None, None, "heads"),
        P("heads", "tok", None, None),
        P("heads", None),
        P(),
        P(),
        P(),
        P(),
        P("heads", None, "tok"),
    )
    return jax.shard_map(
        on_device,
        mesh=mesh,
        in_specs=placed,
        out_specs=(P("heads", "tok", None, None), P(), P("heads", "tok", None, None)),
        check_vma=False,
    )
```

profile of v0, /device:TPU:1, one launch (start us, length us, event | category | flops | bytes accessed | tf_op | source)
XLA Modules:
  0.0 738.8 jit_solution(14970768429014964938)
XLA Ops:
  12.2 89.3 %all-gather.3.cloned.1.call-done = bf16[32,16,32,128]{3,2,1,0:T(8,128)(2,1)} async-done(((bf16[1,16,32,128]{3,2,1,0:T(8,128)(2,1)}), bf16[32,16,32,128]{3,2,1,0:T(8,128)(2,1)}) %all-gather.3.cloned.1.call-update) | async-done | bytes 4194320 | tf_op jit(solution)/shard_map/all_gather | solution.py:100
  101.6 14.7 %reshape_reshape.6 = bf16[32,512,2,64]{3,2,1,0:T(2,128)(2,1)} reshape(bf16[32,16,32,128]{3,2,1,0:T(8,128)(2,1)} %all-gather.3.cloned.1.call-done) | data formatting | bytes 8388608 | tf_op jit(solution)/shard_map/reshape;reshape | solution.py:103
  116.3 18.4 %copy.59 = bf16[32,512,2,64]{1,3,2,0:T(8,128)(2,1)} copy(bf16[32,512,2,64]{3,2,1,0:T(2,128)(2,1)} %reshape_reshape.6) | data formatting | bytes 8388608
  134.7 53.0 %all-gather.5.cloned.1.call-done = bf16[32,16,32,128]{3,2,1,0:T(8,128)(2,1)} async-done(((bf16[1,16,32,128]{3,2,1,0:T(8,128)(2,1)}), bf16[32,16,32,128]{3,2,1,0:T(8,128)(2,1)}) %all-gather.5.cloned.1.call-update) | async-done | bytes 4194320 | tf_op jit(solution)/shard_map/all_gather | solution.py:101
  187.7 14.7 %reshape_reshape.7 = bf16[32,512,2,64]{3,2,1,0:T(2,128)(2,1)} reshape(bf16[32,16,32,128]{3,2,1,0:T(8,128)(2,1)} %all-gather.5.cloned.1.call-done) | data formatting | bytes 8388608 | tf_op jit(solution)/shard_map/reshape;reshape | solution.py:104
  202.4 18.4 %copy.61 = bf16[32,512,2,64]{1,3,2,0:T(8,128)(2,1)} copy(bf16[32,512,2,64]{3,2,1,0:T(2,128)(2,1)} %reshape_reshape.7) | data formatting | bytes 8388608
  220.8 245.2 %while.15 = (s32[]{:T(128)}, f32[512,2]{0,1:T(2,128)S(1)}, f32[512,2]{0,1:T(2,128)S(1)}, f32[512,2,64]{0,2,1:T(8,128)}, bf16[32,512,2,64]{1,3,2,0:T(8,128)(2,1)}...) while((s32[]{:T(128)}, f32[512,2]{0,1:T(2,128)S(1)}, ...), condition=%wide.region_3.4_spmd.clone, body=%wide.region_0.3_spmd.clone.sunk | while | flops 138613760 | bytes 7275625 | solution.py:109
  225.6 2.9 fusion.86
  233.2 2.9 fusion.86
  240.9 2.9 fusion.86
  248.6 2.9 fusion.86
  256.2 2.9 fusion.86
  263.9 2.9 fusion.86
  271.6 2.9 fusion.86
  279.2 2.9 fusion.86
  286.9 2.9 fusion.86
  294.5 2.9 fusion.86
  302.2 2.9 fusion.86
  309.9 2.9 fusion.86
  317.5 2.9 fusion.86
  325.2 2.9 fusion.86
  332.9 2.9 fusion.86
  340.5 2.9 fusion.86
  348.2 2.9 fusion.86
  355.8 2.9 fusion.86
  363.5 2.9 fusion.86
  371.2 2.9 fusion.86
  417.1 2.9 fusion.86
  424.8 2.9 fusion.86
  432.5 2.9 fusion.86
  473.6 34.1 %reduce-scatter.2.cloned.1.call-done = bf16[2,1,32,1024]{3,2,0,1:T(8,128)(2,1)} async-done(((bf16[16,1,32,1024]{3,2,0,1:T(8,128)(2,1)}), bf16[2,1,32,1024]{3,2,0,1:T(8,128)(2,1)}) %reduce-scatter.2.cloned.1.call-update) | async-done | bytes 131088 | tf_op jit(solution)/shard_map/reduce_scatter | solution.py:112
  508.9 25.4 %all_to_all.21 = bf16[2,1,32,1024]{3,0,1,2:T(2,128)(2,1)S(1)} all-to-all(bf16[2,1,32,1024]{3,0,1,2:T(2,128)(2,1)S(1)} %copy.63), channel_id=1, replica_groups=mesh['heads'=8,'tok'=32] {'tok'}, dimensions={2} | all-to-all | bytes 262144 | tf_op jit(solution)/shard_map/all_to_all | solution.py:121
  536.9 4.0 collective-permute-start
  541.8 4.7 collective-permute-start.2
  548.4 5.1 collective-permute-done.3
  556.7 3.3 collective-permute-start.4
  566.1 3.5 collective-permute-start.6
  572.2 4.4 collective-permute-done.7
  582.2 77.4 %all-reduce.4 = (f32[]{:T(128)}, f32[]{:T(128)}) all-reduce(f32[]{:T(128)} %get-tuple-element.93, f32[]{:T(128)S(6)} %add.53), channel_id=1, replica_groups=mesh['heads'=8,'tok'=32] {'heads','tok'}, use_global_device_ids=true, to_apply=%region_6.7 | all-reduce | flops 2 | bytes 16 | tf_op jit(solution)/shard_map/psum | solution.py:135
  663.6 3.2 collective-permute-start.8
  668.1 3.2 collective-permute-done.9
  671.3 6.2 collective-permute-start.10
  679.5 5.1 collective-permute-done.11
  691.1 3.2 collective-permute-done.13
  694.3 3.9 collective-permute-start.14
  700.2 5.1 collective-permute-done.15
  708.1 10.6 %all-to-all-start.1 = ((bf16[2,32,1,1024]{3,0,2,1:T(2,128)(2,1)}), bf16[2,32,1,1024]{3,0,2,1:T(2,128)(2,1)}, u32[]{:S(2)}, u32[]{:S(2)}) async-start(bf16[2,32,1,1024]{3,0,2,1:T(2,128)(2,1)} %copy.79), calls=%async_computation.2 | async-start | bytes 262144 | tf_op jit(solution)/shard_map/all_to_all | solution.py:164
  720.1 9.5 %all-to-all-done.1 = bf16[2,32,1,1024]{3,0,2,1:T(2,128)(2,1)} async-done(((bf16[2,32,1,1024]{3,0,2,1:T(2,128)(2,1)}), bf16[2,32,1,1024]{3,0,2,1:T(2,128)(2,1)}, u32[]{:S(2)}, u32[]{:S(2)}) %all-to-all-start.1) | async-done | bytes 131104 | tf_op jit(solution)/shard_map/all_to_all | solution.py:164
  (382 shorter events, 232.2 us)
Async XLA Ops:
  7.2 547.0 %copy-start = (bf16[3,3,3,256,256]{4,3,2,1,0:T(8,128)(2,1)S(1)}, bf16[3,3,3,256,256]{4,3,2,1,0:T(8,128)(2,1)}, u32[]{:S(2)}) copy-start(bf16[3,3,3,256,256]{4,3,2,1,0:T(8,128)(2,1)} %param.18) | copy-start | bytes 10616836
  7.2 94.4 %all-gather.3.cloned.1.call-start = ((), (), s32[]{:S(2)}) async-start(), calls=%async_computation.3 | async-start | bytes 4325376 | tf_op jit(solution)/shard_map/all_gather | solution.py:100
  7.9 179.8 %all-gather.5.cloned.1.call-start = ((), (), s32[]{:S(2)}) async-start(), calls=%async_computation.4 | async-start | bytes 4325376 | tf_op jit(solution)/shard_map/all_gather | solution.py:101
  8.7 499.1 %reduce-scatter.2.cloned.1.call-start = ((), (), s32[]{:S(2)}) async-start(), calls=%async_computation.5 | async-start | bytes 1179648 | tf_op jit(solution)/shard_map/reduce_scatter | solution.py:112
  508.8 39.7 %copy-start.6 = (bf16[2,1,32,1024]{3,2,0,1:T(8,128)(2,1)}, bf16[2,1,32,1024]{3,2,0,1:T(8,128)(2,1)S(1)}, u32[]{:S(2)}) copy-start(bf16[2,1,32,1024]{3,2,0,1:T(8,128)(2,1)S(1)} %add_convert_fusion) | copy-start | bytes 393220
  535.6 5.3 collective-permute-start.1
  536.9 4.8 collective-permute-start
  541.8 6.6 collective-permute-start.2
  546.5 7.1 collective-permute-start.3
  553.7 7.6 %copy-start.9 = (s32[2,32,1]{1,2,0:T(1,128)S(1)}, s32[2,32,1]{1,2,0:T(1,128)}, u32[]{:S(2)}) copy-start(s32[2,32,1]{1,2,0:T(1,128)} %param.21) | copy-start | bytes 772
  553.7 8.3 %copy-start.11 = (bf16[256]{0:T(256)(128)(2,1)S(1)}, bf16[256]{0:T(256)(128)(2,1)}, u32[]{:S(2)}) copy-start(bf16[256]{0:T(256)(128)(2,1)} %param.20) | copy-start | bytes 1540
  555.5 0.6 copy-start.4
  556.7 7.7 %collective-permute-start.4 = (bf16[1,32,1,256]{3,1,2,0:T(8,128)(2,1)}, bf16[1,32,1,256]{3,1,2,0:T(8,128)(2,1)S(1)}, u32[]{:S(2)}, u32[]{:S(2)}) collective-permute-start(bf16[1,32,1,256]{3,1,2,0:T(8,128)(2,1)} %get-tuple-element.220), channel_id=1, source_target_pairs={{0,32},{32,64},{64,96},{96,128},{128,160},{160,192},{192,224},{1,3... | collective-permute-start | bytes 49160 | tf_op jit(solution)/shard_map/ppermute | solution.py:26
  560.0 5.0 collective-permute-start.5
  564.4 14.3 %copy-start.1 = (bf16[3,3,3,256,256]{4,3,2,1,0:T(8,128)(2,1)S(1)}, bf16[3,3,3,256,256]{4,3,2,1,0:T(8,128)(2,1)}, u32[]{:S(2)}) copy-start(bf16[3,3,3,256,256]{4,3,2,1,0:T(8,128)(2,1)} %param.19) | copy-start | bytes 10616836
  566.1 6.2 collective-permute-start.6
  569.5 7.1 collective-permute-start.7
  577.6 2.5 copy-start.10
  577.6 2.5 copy-start.12
  577.6 85.0 %copy-start.8 = (f32[256]{0:T(256)S(1)}, f32[256]{0:T(256)}, u32[]{:S(2)}) copy-start(f32[256]{0:T(256)} %convert_element_type.83) | copy-start | bytes 3076
  579.4 0.6 copy-start.5
  660.9 25.2 %copy-start.2 = (bf16[3,3,3,256,256]{4,3,2,1,0:T(8,128)(2,1)S(1)}, bf16[3,3,3,256,256]{4,3,2,1,0:T(8,128)(2,1)}, u32[]{:S(2)}) copy-start(bf16[3,3,3,256,256]{4,3,2,1,0:T(8,128)(2,1)} %param.19) | copy-start | bytes 10616836
  660.9 25.2 %copy-start.7 = (f32[64,256]{1,0:T(8,128)S(1)}, f32[64,256]{1,0:T(8,128)}, u32[]{:S(2)}) copy-start(f32[64,256]{1,0:T(8,128)} %get-tuple-element.227) | copy-start | bytes 196612
  663.6 4.5 collective-permute-start.8
  666.8 4.5 collective-permute-start.9
  671.3 8.2 %collective-permute-start.10 = (bf16[4,32,1,256]{3,1,0,2:T(8,128)(2,1)S(1)}, bf16[4,32,1,256]{3,1,0,2:T(8,128)(2,1)S(1)}, u32[]{:S(2)}, u32[]{:S(2)}) collective-permute-start(bf16[4,32,1,256]{3,1,0,2:T(8,128)(2,1)S(1)} %pad_maximum_fusion.2), channel_id=1, source_target_pairs={{0,1},{1,2},{2,3},{3,4},{4,5},{5,6},{6,7},{7,8},{8,9},{9,10},{10,1... | collective-permute-start | bytes 196616 | tf_op jit(solution)/shard_map/ppermute | solution.py:26
  677.5 7.1 collective-permute-start.11
  687.3 3.8 collective-permute-start.12
  689.8 4.5 collective-permute-start.13
  694.3 5.9 collective-permute-start.14
  698.2 7.1 collective-permute-start.15
  705.5 1.6 copy-start.3
  708.1 21.4 %all-to-all-start.1 = ((bf16[2,32,1,1024]{3,0,2,1:T(2,128)(2,1)}), bf16[2,32,1,1024]{3,0,2,1:T(2,128)(2,1)}, u32[]{:S(2)}, u32[]{:S(2)}) async-start(bf16[2,32,1,1024]{3,0,2,1:T(2,128)(2,1)} %copy.79), calls=%async_computation.2 | async-start | bytes 262144 | tf_op jit(solution)/shard_map/all_to_all | solution.py:164
Sparse Core Ops, SparseCore 0:
  10.8 90.7 all-gather.2
  104.4 83.2 all-gather.4
  473.8 33.9 reduce-scatter.1
where the time goes:
time: 744 us; the launch traced here: 739 us
  waiting for transfers between devices  215 us (29%)
  matrix products  191 us (26%)
  blocking collectives  103 us (14%)
  local copies, waits for them, and re-layouts  81.2 us (11%)
  other arithmetic  73.8 us (10%)
  starting transfers between devices  54.8 us (7%)
  between operations  20.2 us (3%)
    dot_general x32, matrix products, online_step(): jnp.einsum('qhk,khd->qhd', raw_weights.astype(jnp.bfloat16), value_block,...  91.5 us
    dot_general x32, matrix products, online_step(): jnp.einsum('qhd,khd->qhk', query_block, key_block, preferred_element_type...  90.1 us
    all_gather x1, waiting for transfers between devices, on_device(): lax.all_gather(key_rows, 'tok', axis=0, tiled=True)  89.3 us
    psum x1, blocking collectives, on_device(): lax.psum((jnp.sum(probability * fault_mask), jnp.sum(probability), jnp.su...  77.4 us
    reduce_sum x32, other arithmetic, online_step(): totals = totals * factor + jnp.sum(raw_weights, axis=-1)  62.5 us
    all_gather x1, waiting for transfers between devices, on_device(): lax.all_gather(value_rows, 'tok', axis=0, tiled=True)  53 us
    unnamed x134, local copies, waits for them, and re-layouts  43.1 us
    reduce_scatter x1, waiting for transfers between devices, on_device(): lax.psum_scatter(jnp.einsum('tzxe,ed->ztxd', attended_grid, w_out, prefer...  34.1 us
  transfers between devices with their start and end apart: 20, of which 12 were waited for; matrix products, arithmetic and copies ran while one was open for 5% of the time, Pallas kernels for 0%

commit v1 on v0

v1 whole, which is shorter than its diff:
```python
import functools

import jax
import jax.numpy as jnp
from jax import lax
from jax.experimental import pallas as pl
from jax.experimental.pallas import tpu as pltpu
from jax.sharding import PartitionSpec as P

MESH = pl.DeviceIdType.MESH
BF = jnp.bfloat16
F32 = jnp.float32
HD = 64
LOSS_SCALE = 64.0
LOG2E = 1.4426950408889634
NN = (((1,), (0,)), ((), ()))
NT = (((1,), (1,)), ((), ()))
TOK = 512
ROWS = 528
NZ = 8
SLOT = {(0, 0): 0, (0, 1): 1}
for _k in (1, 2, 3):
    _b = 4 * _k - 2
    SLOT.update({(-_k, 0): _b, (_k, 0): _b + 1, (-_k, 1): _b + 2, (_k, 1): _b + 3})
SLOT.update({(4, 0): 14, (4, 1): 15})
DISTANCE = [None] * 16
for _key, _slot in SLOT.items():
    DISTANCE[_slot] = _key
TILES = [(0, 1), (2, 3, 4, 5), (6, 7, 8, 9), (10, 11, 12, 13), (14, 15)]


def place():
    heads, tok = lax.axis_index("heads"), lax.axis_index("tok")
    return heads, tok, tok // 4, (tok // 2) % 2, tok % 2


def at(heads, tok):
    return {"heads": heads, "tok": tok}


def attention_kernel(
    q_hbm, k_hbm, v_hbm, lab_hbm, w_hbm,
    out_ref, lab_out, w_full,
    kv, q_buf, qx, acc, peak, o_send, o_recv, lse_send, lse_recv, lab_send, lab_recv, w_buf,
    local_sem, kv_send, kv_recv, mate_send, y_send, y_recv, w_send, w_recv,
):
    heads, tok, z, y, core = place()
    up = at(heads, (tok + 4) % (4 * NZ))
    down = at(heads, (tok + 4 * NZ - 4) % (4 * NZ))
    mate = at(heads, tok + 1 - 2 * core)
    across = at(heads, tok + 2 - 4 * y)
    others = [at((heads + d) % 8, tok) for d in range(1, 8)]

    local = [
        pltpu.make_async_copy(k_hbm, kv.at[0, 0:TOK, 0:128], local_sem.at[0]),
        pltpu.make_async_copy(v_hbm, kv.at[0, 0:TOK, 128:256], local_sem.at[1]),
        pltpu.make_async_copy(lab_hbm, kv.at[0, TOK:ROWS, :], local_sem.at[2]),
        pltpu.make_async_copy(q_hbm, q_buf.at[0], local_sem.at[3]),
        pltpu.make_async_copy(w_hbm, w_buf, local_sem.at[4]),
    ]
    for copy in local:
        copy.start()
    barrier = pltpu.get_barrier_semaphore()
    peers = [up, down, mate, across] + others
    for peer in peers:
        pl.semaphore_signal(barrier, inc=1, device_id=peer, device_id_type=MESH)
    pl.semaphore_wait(barrier, len(peers))
    for copy in local:
        copy.wait()

    sent = []

    def send(src, dst, send_sem, recv_sem, peer):
        copy = pltpu.make_async_remote_copy(
            src_ref=src, dst_ref=dst, send_sem=send_sem, recv_sem=recv_sem, device_id=peer, device_id_type=MESH
        )
        copy.start()
        sent.append(copy)
        return copy

    arrivals = {}
    n_ring = [0]

    def pass_on(distance):
        slot = SLOT[(distance, 0)]
        src = kv.at[slot]

        def ring(to, peer, rows, part):
            dst = SLOT[(to, 0)]
            lo, hi = rows
            copy = send(
                kv.at[slot, lo:hi], kv.at[dst, lo:hi], kv_send.at[n_ring[0]], kv_recv.at[16 * part + dst], peer
            )
            n_ring[0] += 1
            arrivals.setdefault((to, 0), []).append(copy)

        whole = (0, ROWS)
        if distance <= 0 and distance > -3:
            ring(distance - 1, up, whole, 0)
        if distance >= 0 and distance < 3:
            ring(distance + 1, down, whole, 0)
        if distance == -3:
            ring(4, up, (0, 256), 0)
        if distance == 3:
            ring(4, down, (256, ROWS), 1)
        dst = SLOT[(distance, 1)]
        copy = send(src, kv.at[dst], mate_send.at[slot], kv_recv.at[dst], mate)
        arrivals.setdefault((distance, 1), []).append(copy)

    def await_block(key):
        for copy in arrivals[key]:
            copy.wait_recv()

    def prepare(half):
        lane = lax.broadcasted_iota(jnp.int32, (TOK, 128), 1)
        q = q_buf[half].astype(F32) * (HD**-0.5 * LOG2E)
        high = q.astype(BF)
        low = (q - high.astype(F32)).astype(BF)
        zero = jnp.zeros_like(high)
        rows = slice(half * TOK, (half + 1) * TOK)
        for h in range(2):
            mine = (lane < HD) if h == 0 else (lane >= HD)
            qx[h, rows, 0:128] = jnp.where(mine, high, zero)
            qx[h, rows, 128:256] = jnp.where(mine, low, zero)
        acc[rows] = jnp.zeros((TOK, 256), F32)
        peak[:, rows] = jnp.full((2, TOK, 128), -1e30, F32)

    def attend(first, count, slots):
        def body(half, carry):
            rows = pl.ds(pl.multiple_of(half * TOK, TOK), TOK)
            lane = lax.broadcasted_iota(jnp.int32, (TOK, 128), 1)
            k = jnp.concatenate([kv[s, 0:TOK, 0:128] for s in slots], axis=0)
            kk = jnp.concatenate([k, k], axis=1)
            v = jnp.concatenate([kv[s, 0:TOK, 128:256] for s in slots], axis=0)
            vx = jnp.concatenate([v, jnp.ones_like(v)], axis=1)
            scores = [lax.dot_general(qx[h, rows, :], kk, NT, preferred_element_type=F32) for h in range(2)]
            sums, factors = [], []
            for h in range(2):
                old = peak[h, rows, :]
                new = jnp.maximum(old, jnp.max(scores[h], axis=1, keepdims=True))
                peak[h, rows, :] = new
                factors.append(jnp.exp2(old - new))
                mixing = jnp.exp2(scores[h] - new[:, :1]).astype(BF)
                sums.append(lax.dot_general(mixing, vx, NN, preferred_element_type=F32))
            factor = jnp.where(lane < HD, factors[0], factors[1])
            for part in (slice(0, 128), slice(128, 256)):
                acc[rows, part] = acc[rows, part] * factor + jnp.where(lane < HD, sums[0][:, part], sums[1][:, part])
            return carry

        lax.fori_loop(first, first + count, body, 0)

    def finish(half):
        lane = lax.broadcasted_iota(jnp.int32, (TOK, 128), 1)
        rows = slice(half * TOK, (half + 1) * TOK)
        total = acc[rows, 128:256]
        top = jnp.where(lane < HD, peak[0, rows], peak[1, rows])
        return acc[rows, 0:128] / total, top + jnp.log(total) * LOG2E

    pass_on(0)
    q_copy = send(q_buf.at[0], q_buf.at[1], y_send.at[0], y_recv.at[0], across)
    prepare(0)
    await_block((0, 1))
    attend(0, 1, TILES[0])
    q_copy.wait_recv()
    prepare(1)
    attend(1, 1, TILES[0])

    my_rows = w_full.at[pl.ds(pl.multiple_of(heads * 128, 128), 128), :]
    own_w = pltpu.make_async_copy(w_buf, my_rows, local_sem.at[5])
    own_w.start()
    w_copies = [send(w_buf, my_rows, w_send.at[d], w_recv.at[d], others[d]) for d in range(7)]

    for k in (1, 2, 3):
        for distance in (-k, k):
            await_block((distance, 0))
            pass_on(distance)
        for distance in (-k, k):
            await_block((distance, 1))
        if k < 3:
            attend(0, 2, TILES[k])
    attend(1, 1, TILES[3])
    await_block((4, 0))
    mate_slot = SLOT[(4, 1)]
    last = send(kv.at[SLOT[(4, 0)]], kv.at[mate_slot], mate_send.at[14], kv_recv.at[mate_slot], mate)
    last.wait_recv()
    attend(1, 1, TILES[4])

    part, lse = finish(1)
    o_send[...] = part.astype(BF)
    flat = lse.T
    lse_send[0:8] = flat[0:8]
    lse_send[8:16] = flat[64:72]
    label_rows = jnp.concatenate([kv[s, TOK:ROWS, :] for s in range(16)], axis=0)
    row = lax.broadcasted_iota(jnp.int32, (64, 256), 0)
    col = lax.broadcasted_iota(jnp.int32, (64, 256), 1)
    pick = jnp.zeros((64, 256), jnp.bool_)
    for s, (distance, other) in enumerate(DISTANCE):
        owner_core = core if other == 0 else 1 - core
        owner = ((z + distance + NZ) % NZ) * 4 + y * 2 + owner_core
        pick = pick | (((row % 32) == owner) & (col == 16 * s + row // 32))
    by_depth = lax.dot_general(
        jnp.where(pick, 1.0, 0.0).astype(BF), label_rows, NN, preferred_element_type=F32
    )
    tok_across = tok + 2 - 4 * y
    lane64 = lax.broadcasted_iota(jnp.int32, (64, 256), 1)

    def at_depth(depth):
        chosen = jnp.sum(jnp.where(lane64 == depth, by_depth, 0.0), axis=1, keepdims=True)
        return jnp.broadcast_to(chosen, (64, 128))

    lab_send[...] = at_depth(tok_across)
    o_copy = send(o_send, o_recv, y_send.at[1], y_recv.at[1], across)
    lse_copy = send(lse_send, lse_recv, y_send.at[2], y_recv.at[2], across)
    lab_copy = send(lab_send, lab_recv, y_send.at[3], y_recv.at[3], across)
    attend(0, 1, TILES[3])
    attend(0, 1, TILES[4])
    mine, my_lse = finish(0)
    o_copy.wait_recv()
    lse_copy.wait_recv()
    lab_copy.wait_recv()
    head0 = jnp.broadcast_to(lse_recv[0:1], (64, TOK))
    head1 = jnp.broadcast_to(lse_recv[8:9], (64, TOK))
    its_lse = jnp.concatenate([head0, head1], axis=0).T
    top = jnp.maximum(my_lse, its_lse)
    my_share, its_share = jnp.exp2(my_lse - top), jnp.exp2(its_lse - top)
    merged = (my_share * mine + its_share * o_recv[...].astype(F32)) / (my_share + its_share)
    out_ref[...] = merged.astype(BF)
    lab_out[...] = at_depth(tok) + lab_recv[...]
    own_w.wait()
    for copy in w_copies:
        copy.wait_recv()
    for copy in sent:
        copy.wait_send()


def attention(queries, key_rows, value_rows, label_rows, w_out):
    dma = pltpu.SemaphoreType.DMA
    return pl.pallas_call(
        attention_kernel,
        out_shape=(
            jax.ShapeDtypeStruct((TOK, 128), BF),
            jax.ShapeDtypeStruct((64, 128), F32),
            jax.ShapeDtypeStruct((1024, 1024), BF),
        ),
        in_specs=[pl.BlockSpec(memory_space=pl.ANY)] * 5,
        out_specs=(
            pl.BlockSpec(memory_space=pltpu.VMEM),
            pl.BlockSpec(memory_space=pltpu.VMEM),
            pl.BlockSpec(memory_space=pl.ANY),
        ),
        scratch_shapes=[
            pltpu.VMEM((16, ROWS, 256), BF),
            pltpu.VMEM((2, TOK, 128), BF),
            pltpu.VMEM((2, 2 * TOK, 256), BF),
            pltpu.VMEM((2 * TOK, 256), F32),
            pltpu.VMEM((2, 2 * TOK, 128), F32),
            pltpu.VMEM((TOK, 128), BF),
            pltpu.VMEM((TOK, 128), BF),
            pltpu.VMEM((16, TOK), F32),
            pltpu.VMEM((16, TOK), F32),
            pltpu.VMEM((64, 128), F32),
            pltpu.VMEM((64, 128), F32),
            pltpu.VMEM((128, 1024), BF),
            dma((6,)),
            dma((8,)),
            dma((32,)),
            dma((16,)),
            dma((4,)),
            dma((4,)),
            dma((7,)),
            dma((7,)),
        ],
        compiler_params=pltpu.CompilerParams(
            collective_id=0, has_side_effects=True, vmem_limit_bytes=58 << 20
        ),
        name="attention",
    )(queries, key_rows, value_rows, label_rows, w_out)


NEAR = [(dh, dt) for dh in (-1, 0, 1) for dt in (-1, 0, 1) if (dh, dt) != (0, 0)]


def decoder_kernel(
    att_ref, lab_ref, wf_hbm, res_ref, neck_hbm, first_hbm, second_hbm, class_ref,
    enc_ref, loss_ref, grad_ref,
    att_all, wf, neck, first, second, halo_one, halo_two, halo_three, halo_four, grad_two,
    stat_a, stat_b, send_a, send_b,
    local_sem, a_send, a_recv, h_send, h_recv, s_send, s_recv, r_send, r_recv,
):
    heads, tok, z, y, core = place()
    loads = [
        pltpu.make_async_copy(src, dst, local_sem.at[i])
        for i, (src, dst) in enumerate(
            ((wf_hbm, wf), (neck_hbm, neck), (first_hbm, first), (second_hbm, second))
        )
    ]
    mine = pl.ds(pl.multiple_of(heads * 128, 128), 128)
    own_rows = pl.ds(pl.multiple_of(heads * 64, 64), 64)
    own = pltpu.make_async_copy(att_ref.at[own_rows], att_all.at[:, mine], local_sem.at[4])
    own.start()
    for load in loads:
        load.start()

    by_head = [at((heads + d) % 8, tok) for d in range(1, 8)]
    near = [at((heads + dh + 8) % 8, (tok + dt + 32) % 32) for dh, dt in NEAR]
    group_a = [
        at((heads + d // 2) % 8, tok if d % 2 == 0 else tok + 1 - 2 * core) for d in range(1, 16)
    ]
    group_b = [
        at(heads, (tok + 4 * (d // 2)) % 32 if d % 2 == 0 else (tok + 4 * (d // 2) + 2 - 4 * y + 32) % 32)
        for d in range(1, 16)
    ]
    peers = by_head + near + group_a + group_b
    barrier = pltpu.get_barrier_semaphore()
    for peer in peers:
        pl.semaphore_signal(barrier, inc=1, device_id=peer, device_id_type=MESH)
    pl.semaphore_wait(barrier, len(peers))

    sent = []

    def send(src, dst, send_sem, recv_sem, peer):
        copy = pltpu.make_async_remote_copy(
            src_ref=src, dst_ref=dst, send_sem=send_sem, recv_sem=recv_sem, device_id=peer, device_id_type=MESH
        )
        copy.start()
        sent.append(copy)
        return copy

    copies = []
    for i in range(7):
        theirs = lax.rem(heads + i + 1, 8)
        copies.append(
            send(
                att_ref.at[pl.ds(pl.multiple_of(theirs * 64, 64), 64)],
                att_all.at[:, mine],
                a_send.at[i],
                a_recv.at[i],
                by_head[i],
            )
        )

    def start_halo(stage, halo):
        halves = []
        for i, (dh, dt) in enumerate(NEAR):
            src, dst = {0: ((32, 96), (32, 96)), 1: ((64, 96), (0, 32)), -1: ((32, 64), (96, 128))}[dh]
            halves.append(
                send(
                    halo.at[1, src[0] : src[1]],
                    halo.at[1 - dt, dst[0] : dst[1]],
                    h_send.at[stage, i],
                    h_recv.at[stage, i],
                    near[i],
                )
            )
        return halves

    def end_halo(halo, halves):
        width = halo.shape[2]
        for copy in halves:
            copy.wait_recv()

        @pl.when(heads == 0)
        def _():
            halo[:, 0:32] = jnp.zeros((3, 32, width), BF)

        @pl.when(heads == 7)
        def _():
            halo[:, 96:128] = jnp.zeros((3, 32, width), BF)

        @pl.when(tok == 0)
        def _():
            halo[0] = jnp.zeros((128, width), BF)

        @pl.when(tok == 31)
        def _():
            halo[2] = jnp.zeros((128, width), BF)

    inline = lax.broadcasted_iota(jnp.int32, (64, 256), 0) % 32

    def conv(halo, weights, flipped):
        parts = []
        for e in range(3):
            total = None
            for a in range(3):
                for b in range(3):
                    c, t = (2 - a, 2 - b) if flipped else (a, b)
                    term = lax.dot_general(
                        halo[t, 32 * c : 32 * c + 64],
                        weights[(a * 3 + b) * 3 + e],
                        NT if flipped else NN,
                        preferred_element_type=F32,
                    )
                    total = term if total is None else total + term
            parts.append(total)
        if flipped:
            parts = parts[::-1]
        before = jnp.where(inline == 0, 0.0, pltpu.roll(parts[0], 1, 0))
        after = jnp.where(inline == 31, 0.0, pltpu.roll(parts[2], 63, 0))
        return before + parts[1] + after

    def sigmoid(v):
        return 1.0 / (1.0 + jnp.exp(-v))

    own.wait()
    loads[0].wait()
    loads[1].wait()
    for copy in copies:
        copy.wait_recv()
    projected = lax.dot_general(att_all[...], wf[...], NN, preferred_element_type=F32)
    encoded = (res_ref[...].astype(F32) + projected).astype(BF)
    enc_ref[...] = encoded
    halo_one[1, 32:96] = lax.dot_general(encoded, neck[...], NN, preferred_element_type=F32).astype(BF)
    halves = start_halo(0, halo_one)
    loads[2].wait()
    end_halo(halo_one, halves)
    hidden_one = conv(halo_one, first, False)
    gate_one = sigmoid(hidden_one)
    halo_two[1, 32:96] = (hidden_one * gate_one).astype(BF)
    halves = start_halo(1, halo_two)
    slope_one = gate_one * (1.0 + hidden_one * (1.0 - gate_one))
    loads[3].wait()
    end_halo(halo_two, halves)
    hidden_two = conv(halo_two, second, False)
    gate_two = sigmoid(hidden_two)
    active_two = (hidden_two * gate_two).astype(BF).astype(F32)
    w_class = class_ref[0:1].astype(F32)
    logits = jnp.sum(active_two * w_class, axis=1, keepdims=True)
    probability = jnp.broadcast_to(sigmoid(logits), (64, 128))
    labels = lab_ref[...]

    def over_cells(value):
        return jnp.sum(value, axis=0, keepdims=True)

    row8 = lax.broadcasted_iota(jnp.int32, (8, 128), 0)
    stats = jnp.where(
        row8 == 0,
        over_cells(probability * labels),
        jnp.where(row8 == 1, over_cells(probability), over_cells(labels)),
    )
    index_a = heads * 2 + core
    send_a[...] = stats
    stat_copies = [
        send(send_a, stat_a.at[index_a], s_send.at[d], s_recv.at[d], group_a[d]) for d in range(15)
    ]
    stat_a[index_a] = stats
    spread = probability * (1.0 - probability)
    slope_two = gate_two * (1.0 + hidden_two * (1.0 - gate_two))
    unscaled = jnp.concatenate([spread, spread], axis=1) * w_class * slope_two
    halo_three[1, 32:96, 0:256] = unscaled.astype(BF)
    halo_three[1, 32:96, 256:384] = labels.astype(BF)
    halves = start_halo(2, halo_three)
    for copy in stat_copies:
        copy.wait_recv()
    partial = stat_a[0]
    for i in range(1, 16):
        partial = partial + stat_a[i]
    index_b = z * 2 + y
    send_b[...] = partial
    stat_copies = [
        send(send_b, stat_b.at[index_b], r_send.at[d], r_recv.at[d], group_b[d]) for d in range(15)
    ]
    stat_b[index_b] = partial
    end_halo(halo_three, halves)
    for copy in stat_copies:
        copy.wait_recv()
    sums = stat_b[0]
    for i in range(1, 16):
        sums = sums + stat_b[i]
    intersection, denominator = sums[0:1], sums[1:2] + sums[2:3]
    loss_ref[...] = jnp.broadcast_to(1.0 - 2.0 * intersection / denominator, (8, 128))
    scale = LOSS_SCALE * 16384.0 * -2.0 / (denominator * denominator)
    for t in range(3):
        cells = halo_three[t, :, 256:384].astype(F32)
        factor = scale * (cells * denominator - intersection)
        factor = jnp.concatenate([factor, factor], axis=1)
        grad_two[t] = (halo_three[t, :, 0:256].astype(F32) * factor).astype(BF)
    grad_active = conv(grad_two, second, True)
    halo_four[1, 32:96] = (grad_active * slope_one).astype(BF)
    halves = start_halo(3, halo_four)
    end_halo(halo_four, halves)
    grad_neck = conv(halo_four, first, True).astype(BF)
    grad_ref[...] = lax.dot_general(grad_neck, neck[...], NT, preferred_element_type=F32).astype(BF)
    for copy in sent:
        copy.wait_send()


def decoder(attended, labels, w_full, residual, w_neck, w_first, w_second, w_class):
    dma = pltpu.SemaphoreType.DMA
    vmem, anywhere = pl.BlockSpec(memory_space=pltpu.VMEM), pl.BlockSpec(memory_space=pl.ANY)
    return pl.pallas_call(
        decoder_kernel,
        out_shape=(
            jax.ShapeDtypeStruct((64, 1024), BF),
            jax.ShapeDtypeStruct((8, 128), F32),
            jax.ShapeDtypeStruct((64, 1024), BF),
        ),
        in_specs=[vmem, vmem, anywhere, vmem, anywhere, anywhere, anywhere, vmem],
        out_specs=(vmem, vmem, vmem),
        scratch_shapes=[
            pltpu.VMEM((64, 1024), BF),
            pltpu.VMEM((1024, 1024), BF),
            pltpu.VMEM((1024, 256), BF),
            pltpu.VMEM((27, 256, 256), BF),
            pltpu.VMEM((27, 256, 256), BF),
            pltpu.VMEM((3, 128, 256), BF),
            pltpu.VMEM((3, 128, 256), BF),
            pltpu.VMEM((3, 128, 384), BF),
            pltpu.VMEM((3, 128, 256), BF),
            pltpu.VMEM((3, 128, 256), BF),
            pltpu.VMEM((16, 8, 128), F32),
            pltpu.VMEM((16, 8, 128), F32),
            pltpu.VMEM((8, 128), F32),
            pltpu.VMEM((8, 128), F32),
            dma((5,)),
            dma((7,)),
            dma((7,)),
            dma((4, 8)),
            dma((4, 8)),
            dma((15,)),
            dma((15,)),
            dma((15,)),
            dma((15,)),
        ],
        compiler_params=pltpu.CompilerParams(
            collective_id=1, has_side_effects=True, vmem_limit_bytes=40 << 20
        ),
        name="decoder",
    )(attended, labels, w_full, residual, w_neck, w_first, w_second, w_class)


def on_device(
    queries, key_rows, value_rows, residual, w_out, w_neck, w_first, w_second, w_class, labels
):
    label_rows = jnp.pad(labels.reshape(2, 32).astype(BF), ((0, 14), (0, 224)))
    attended, own_labels, w_full = attention(
        queries.reshape(TOK, 128), key_rows.reshape(TOK, 128), value_rows.reshape(TOK, 128), label_rows, w_out
    )
    encoded, loss, grad = decoder(
        attended,
        own_labels,
        w_full,
        residual.reshape(64, 1024),
        w_neck,
        w_first.reshape(27, 256, 256),
        w_second.reshape(27, 256, 256),
        jnp.broadcast_to(w_class[None, :], (16, 256)),
    )
    shape = residual.shape
    return (encoded.reshape(shape), loss[0, 0], grad.reshape(shape))


def solution(mesh):
    slab = P("tok", None, None, "heads")
    rows = P("heads", "tok", None, None)
    placed = (slab, slab, slab, rows, P("heads", None), P(), P(), P(), P(), P("heads", None, "tok"))
    return jax.shard_map(
        on_device, mesh=mesh, in_specs=placed, out_specs=(rows, P(), rows), check_vma=False
    )
```

time: 744 us -> 108 us (0.15)
  waiting for transfers between devices: 215 us -> 0 us
  matrix products: 191 us -> 0 us
  blocking collectives: 103 us -> 0 us
  Pallas kernels: 0 us -> 94.3 us
  other arithmetic: 73.8 us -> 0.68 us
  local copies, waits for them, and re-layouts: 81.2 us -> 12.3 us
  starting transfers between devices: 54.8 us -> 0 us
  between operations: 20.2 us -> 0.66 us
    dot_general x72 -> x0, matrix products: 191 us -> none  [the longest x32 91.5 us: online_step(): jnp.einsum('qhk,khd->qhd', raw_weights.astype(jnp.bfloat16), value_block,...]
    all_gather x2 -> x0, waiting for transfers between devices: 142 us -> none  [the longest x1 89.3 us: on_device(): lax.all_gather(key_rows, 'tok', axis=0, tiled=True)]
    pallas_call x0 -> x2, Pallas kernels: none -> 94.3 us  [the longest x1 51.9 us: attention(): pl.pallas_call(attention_kernel, out_shape=(jax.ShapeDtypeStruct((TOK, 12...]
    psum x1 -> x0, blocking collectives: 77.4 us -> none  [on_device(): lax.psum((jnp.sum(probability * fault_mask), jnp.sum(probability), jnp.su...]
    reduce_sum x33 -> x0, other arithmetic: 63.2 us -> none  [the longest x32 62.5 us: online_step(): totals = totals * factor + jnp.sum(raw_weights, axis=-1)]
    ppermute x16 -> x0, starting transfers between devices: 44.1 us -> none  [the longest x8 31.2 us: padded_2(): before = lax.ppermute(last, axis, up)]
    reduce_scatter x1 -> x0, waiting for transfers between devices: 34.1 us -> none  [on_device(): lax.psum_scatter(jnp.einsum('tzxe,ed->ztxd', attended_grid, w_out, prefer...]
    unnamed x134 -> x17, local copies, waits for them, and re-layouts: 43.1 us -> 10.5 us
  transfers between devices with their start and end apart: 20 -> 0, of which waited for: 12 -> 0; matrix products, arithmetic and copies ran while one was open for 5% -> 0% of each run, Pallas kernels for 0% -> 0%
where the time goes in v1:
time: 108 us
  Pallas kernels  94.3 us (87%)
  local copies, waits for them, and re-layouts  12.3 us (11%)
    pallas_call x1, Pallas kernels, attention(): pl.pallas_call(attention_kernel, out_shape=(jax.ShapeDtypeStruct((TOK, 12...  51.9 us
    pallas_call x1, Pallas kernels, decoder(): pl.pallas_call(decoder_kernel, out_shape=(jax.ShapeDtypeStruct((64, 1024)...  42.4 us
    unnamed x17, local copies, waits for them, and re-layouts  10.5 us

profile of v1, /device:TPU:1, one launch (start us, length us, event | category | flops | bytes accessed | tf_op | source)
XLA Modules:
  0.0 108.0 jit_solution(8054809769826982107)
XLA Ops:
  0.6 0.7 convert_element_type.8
  1.3 0.6 pad.4.lab_hbm
  1.9 0.7 broadcast_in_dim.2.class_ref
  2.6 51.9 %attention.1 = (bf16[512,128]{1,0:T(8,128)(2,1)}, f32[64,128]{1,0:T(8,128)}, bf16[1024,1024]{1,0:T(8,128)(2,1)}) custom-call(bf16[512,128]{1,0:T(8,128)(2,1)} %bitcast.21, bf16[512,128]{1,0:T(8,128)(2,1)} %bitcast.22, bf16[512,128]{1,0:T(8,128)(2,1)} %bitcast.23, bf16[16,256]{1,0:T(8,128)(2,1)} %pad.4.lab_hbm, bf16[128,1024]{1,0:T(8,128)(2,1)} %w_hbm.1), custom_call_target="tpu_custom_call" | custom-call | tf_op jit(solution)/shard_map/attention/pallas_call | solution.py:238
  54.5 0.0 copy-start
  54.5 2.0 %copy-done = bf16[3,3,3,256,256]{4,3,2,1,0:T(8,128)(2,1)S(1)} copy-done((bf16[3,3,3,256,256]{4,3,2,1,0:T(8,128)(2,1)S(1)}, bf16[3,3,3,256,256]{4,3,2,1,0:T(8,128)(2,1)}, u32[]{:S(2)}) %copy-start) | copy-done | bytes 3538968
  56.5 0.0 copy-start.1
  56.5 2.0 %copy-done.1 = bf16[3,3,3,256,256]{4,3,2,1,0:T(8,128)(2,1)S(1)} copy-done((bf16[3,3,3,256,256]{4,3,2,1,0:T(8,128)(2,1)S(1)}, bf16[3,3,3,256,256]{4,3,2,1,0:T(8,128)(2,1)}, u32[]{:S(2)}) %copy-start.1) | copy-done | bytes 3538968
  58.5 0.0 copy-start.2
  58.5 1.6 %copy-done.2 = bf16[1024,1024]{1,0:T(8,128)(2,1)S(1)} copy-done((bf16[1024,1024]{1,0:T(8,128)(2,1)S(1)}, bf16[1024,1024]{1,0:T(8,128)(2,1)}, u32[]{:S(2)}) %copy-start.2) | copy-done | bytes 2097176
  60.1 0.0 copy-start.3
  60.1 1.0 copy-done.3
  61.2 0.0 copy-start.4
  61.2 0.9 copy-done.4
  62.1 0.0 copy-start.5
  62.1 0.9 copy-done.5
  63.0 0.0 copy-start.6
  63.0 0.8 copy-done.6
  63.7 42.4 %decoder.1 = (bf16[64,1024]{1,0:T(8,128)(2,1)S(1)}, f32[8,128]{1,0:T(8,128)S(1)}, bf16[64,1024]{1,0:T(8,128)(2,1)S(1)}) custom-call(bf16[512,128]{1,0:T(8,128)(2,1)S(1)} %copy-done.5, f32[64,128]{1,0:T(8,128)S(1)} %copy-done.6, bf16[1024,1024]{1,0:T(8,128)(2,1)S(1)} %copy-done.2, bf16[64,1024]{1,0:T(8,128)(2,1)S(1)} %bitcast.18, ...), custom_call_target="tpu_custom_call" | custom-call | tf_op jit(solution)/shard_map/decoder/pallas_call | solution.py:490
  106.1 0.5 slice.3
  106.6 0.7 copy.20
  107.3 0.7 copy.21
  (1 shorter events, 0.0 us)
Async XLA Ops:
  54.5 2.0 %copy-start = (bf16[3,3,3,256,256]{4,3,2,1,0:T(8,128)(2,1)S(1)}, bf16[3,3,3,256,256]{4,3,2,1,0:T(8,128)(2,1)}, u32[]{:S(2)}) copy-start(bf16[3,3,3,256,256]{4,3,2,1,0:T(8,128)(2,1)} %param.16) | copy-start | bytes 10616836
  56.5 2.0 %copy-start.1 = (bf16[3,3,3,256,256]{4,3,2,1,0:T(8,128)(2,1)S(1)}, bf16[3,3,3,256,256]{4,3,2,1,0:T(8,128)(2,1)}, u32[]{:S(2)}) copy-start(bf16[3,3,3,256,256]{4,3,2,1,0:T(8,128)(2,1)} %param.17) | copy-start | bytes 10616836
  58.5 1.6 %copy-start.2 = (bf16[1024,1024]{1,0:T(8,128)(2,1)S(1)}, bf16[1024,1024]{1,0:T(8,128)(2,1)}, u32[]{:S(2)}) copy-start(bf16[1024,1024]{1,0:T(8,128)(2,1)} %get-tuple-element.11.wf_hbm) | copy-start | bytes 6291460
  60.1 1.0 copy-start.3
  61.2 0.9 copy-start.4
  62.1 0.9 copy-start.5
  63.0 0.8 copy-start.6

commit v2 on v1

v2 whole, which is shorter than its diff:
```python
import jax
import jax.numpy as jnp
from jax import lax
from jax.experimental import pallas as pl
from jax.experimental.pallas import tpu as pltpu
from jax.sharding import PartitionSpec as P

MESH = pl.DeviceIdType.MESH
BF = jnp.bfloat16
F32 = jnp.float32
HD = 64
LOSS_SCALE = 64.0
LOG2E = 1.4426950408889634
NN = (((1,), (0,)), ((), ()))
NT = (((1,), (1,)), ((), ()))
TOK = 512
ROWS = 528
NZ = 8
SLOT = {(0, 0): 0, (0, 1): 1}
for _k in (1, 2, 3):
    _b = 4 * _k - 2
    SLOT.update({(-_k, 0): _b, (_k, 0): _b + 1, (-_k, 1): _b + 2, (_k, 1): _b + 3})
SLOT.update({(4, 0): 14, (4, 1): 15})
DISTANCE = [None] * 16
for _key, _slot in SLOT.items():
    DISTANCE[_slot] = _key
TILES = [(0, 1), (2, 3, 4, 5), (6, 7, 8, 9), (10, 11, 12, 13), (14, 15)]


def place():
    heads, tok = lax.axis_index("heads"), lax.axis_index("tok")
    return heads, tok, tok // 4, (tok // 2) % 2, tok % 2


def at(heads, tok):
    return {"heads": heads, "tok": tok}


NEAR = [(dh, dt) for dh in (-1, 0, 1) for dt in (-1, 0, 1) if (dh, dt) != (0, 0)]
PARTS = ((0, TOK // 2), (TOK // 2, ROWS))


def block_kernel(
    q_hbm, k_hbm, v_hbm, lab_ref, w_hbm, res_hbm, neck_hbm, first_hbm, second_hbm, class_hbm,
    enc_hbm, loss_ref, grad_hbm,
    kv, q_buf, qx, acc, peak, o_send, o_recv, lse_send, lse_recv, lab_send, lab_recv, attended,
    att_all, wf, neck, first, second, residual, w_class_buf, result,
    halo_one, halo_two, halo_three, halo_four, grad_two, stat_a, stat_b, send_a, send_b,
    local_sem, kv_send, kv_recv, mate_send, y_send, y_recv, w_send, w_recv,
    a_send, a_recv, h_send, h_recv, s_send, s_recv, r_send, r_recv,
):
    heads, tok, z, y, core = place()
    up = at(heads, (tok + 4) % (4 * NZ))
    down = at(heads, (tok + 4 * NZ - 4) % (4 * NZ))
    mate = at(heads, tok + 1 - 2 * core)
    across = at(heads, tok + 2 - 4 * y)
    others = [at((heads + d) % 8, tok) for d in range(1, 8)]
    near = [at((heads + dh + 8) % 8, (tok + dt + 32) % 32) for dh, dt in NEAR]
    group_a = [
        at((heads + d // 2) % 8, tok if d % 2 == 0 else tok + 1 - 2 * core) for d in range(1, 16)
    ]
    group_b = [
        at(heads, (tok + 4 * (d // 2)) % 32 if d % 2 == 0 else (tok + 4 * (d // 2) + 2 - 4 * y + 32) % 32)
        for d in range(1, 16)
    ]
    mine = pl.ds(pl.multiple_of(heads * 128, 128), 128)
    own_rows = pl.ds(pl.multiple_of(heads * 64, 64), 64)

    local = [
        pltpu.make_async_copy(k_hbm, kv.at[0, 0:TOK, 0:128], local_sem.at[0]),
        pltpu.make_async_copy(v_hbm, kv.at[0, 0:TOK, 128:256], local_sem.at[1]),
        pltpu.make_async_copy(q_hbm, q_buf.at[0], local_sem.at[2]),
        pltpu.make_async_copy(w_hbm, wf.at[mine], local_sem.at[3]),
    ]
    loads = [
        pltpu.make_async_copy(src, dst, local_sem.at[4 + i])
        for i, (src, dst) in enumerate(
            (
                (neck_hbm, neck),
                (first_hbm, first),
                (second_hbm, second),
                (res_hbm, residual),
                (class_hbm, w_class_buf),
            )
        )
    ]
    for copy in local:
        copy.start()
    barrier = pltpu.get_barrier_semaphore()
    peers = [up, down, mate, across] + others
    for peer in peers:
        pl.semaphore_signal(barrier, inc=1, device_id=peer, device_id_type=MESH)
    lab_rows = jnp.concatenate(
        [lab_ref[...].astype(F32), jnp.zeros((2, 224), F32)], axis=1
    )
    lab_rows = jnp.concatenate([lab_rows, jnp.zeros((14, 256), F32)], axis=0)
    kv[0, TOK:ROWS, :] = lab_rows.astype(BF)
    pl.semaphore_wait(barrier, len(peers))
    for copy in local:
        copy.wait()

    sent = []

    def send(src, dst, send_sem, recv_sem, peer):
        copy = pltpu.make_async_remote_copy(
            src_ref=src, dst_ref=dst, send_sem=send_sem, recv_sem=recv_sem, device_id=peer, device_id_type=MESH
        )
        copy.start()
        sent.append(copy)
        return copy

    arrivals = {}
    n_ring = [0]

    def ring(distance, part):
        slot = SLOT[(distance, 0)]
        lo, hi = PARTS[part]
        for step, peer in ((-1, up), (1, down)):
            if distance * step < 0:
                continue
            to = distance + step
            if abs(to) > 3:
                if part != (0 if step < 0 else 1):
                    continue
                to = 4
            dst = SLOT[(to, 0)]
            copy = send(
                kv.at[slot, lo:hi], kv.at[dst, lo:hi], kv_send.at[n_ring[0]], kv_recv.at[2 * dst + part], peer
            )
            n_ring[0] += 1
            arrivals[(to, 0, part)] = copy

    def share(distance, part):
        slot, dst = SLOT[(distance, 0)], SLOT[(distance, 1)]
        lo, hi = PARTS[part]
        arrivals[(distance, 1, part)] = send(
            kv.at[slot, lo:hi],
            kv.at[dst, lo:hi],
            mate_send.at[2 * slot + part],
            kv_recv.at[2 * dst + part],
            mate,
        )

    def arrive(k, part):
        for distance in (-k, k):
            arrivals[(distance, 0, part)].wait_recv()
            ring(distance, part)
            share(distance, part)

    def await_mate(*distances):
        for distance in distances:
            for part in range(2):
                arrivals[(distance, 1, part)].wait_recv()

    def prepare(half):
        lane = lax.broadcasted_iota(jnp.int32, (TOK, 128), 1)
        q = q_buf[half].astype(F32) * (HD**-0.5 * LOG2E)
        high = q.astype(BF)
        low = (q - high.astype(F32)).astype(BF)
        zero = jnp.zeros_like(high)
        rows = slice(half * TOK, (half + 1) * TOK)
        for h in range(2):
            mine_h = (lane < HD) if h == 0 else (lane >= HD)
            qx[h, rows, 0:128] = jnp.where(mine_h, high, zero)
            qx[h, rows, 128:256] = jnp.where(mine_h, low, zero)
        acc[rows] = jnp.zeros((TOK, 256), F32)
        peak[:, rows] = jnp.full((2, TOK, 128), -1e30, F32)

    def attend(half, slots):
        rows = slice(half * TOK, (half + 1) * TOK)
        lane = lax.broadcasted_iota(jnp.int32, (TOK, 128), 1)
        k = jnp.concatenate([kv[s, 0:TOK, 0:128] for s in slots], axis=0)
        kk = jnp.concatenate([k, k], axis=1)
        v = jnp.concatenate([kv[s, 0:TOK, 128:256] for s in slots], axis=0)
        vx = jnp.concatenate([v, jnp.ones_like(v)], axis=1)
        scores = [lax.dot_general(qx[h, rows, :], kk, NT, preferred_element_type=F32) for h in range(2)]
        sums, factors = [], []
        for h in range(2):
            old = peak[h, rows, :]
            new = jnp.maximum(old, jnp.max(scores[h], axis=1, keepdims=True))
            peak[h, rows, :] = new
            factors.append(jnp.exp2(old - new))
            mixing = jnp.exp2(scores[h] - new[:, :1]).astype(BF)
            sums.append(lax.dot_general(mixing, vx, NN, preferred_element_type=F32))
        factor = jnp.where(lane < HD, factors[0], factors[1])
        for part in (slice(0, 128), slice(128, 256)):
            acc[rows, part] = acc[rows, part] * factor + jnp.where(lane < HD, sums[0][:, part], sums[1][:, part])

    def finish(half):
        lane = lax.broadcasted_iota(jnp.int32, (TOK, 128), 1)
        rows = slice(half * TOK, (half + 1) * TOK)
        total = acc[rows, 128:256]
        top = jnp.where(lane < HD, peak[0, rows], peak[1, rows])
        return acc[rows, 0:128] / total, top + jnp.log(total) * LOG2E

    q_copy = send(q_buf.at[0], q_buf.at[1], y_send.at[0], y_recv.at[0], across)
    for part in range(2):
        ring(0, part)
    for part in range(2):
        share(0, part)
    prepare(0)
    await_mate(0)
    attend(0, TILES[0])
    w_copies = [send(wf.at[mine], wf.at[mine], w_send.at[d], w_recv.at[d], others[d]) for d in range(7)]
    for load in loads:
        load.start()
    q_copy.wait_recv()
    prepare(1)
    arrive(1, 0)
    attend(1, TILES[0])
    arrive(1, 1)
    await_mate(-1, 1)
    attend(0, TILES[1])
    arrive(2, 0)
    attend(1, TILES[1])
    arrive(2, 1)
    await_mate(-2, 2)
    attend(0, TILES[2])
    arrive(3, 0)
    attend(1, TILES[2])
    arrive(3, 1)
    await_mate(-3, 3)
    attend(1, TILES[3])
    for part in range(2):
        arrivals[(4, 0, part)].wait_recv()
        share(4, part)
    await_mate(4)
    attend(1, TILES[4])

    part, lse = finish(1)
    o_send[...] = part.astype(BF)
    flat = lse.T
    lse_send[0:8] = flat[0:8]
    lse_send[8:16] = flat[64:72]
    label_rows = jnp.concatenate([kv[s, TOK:ROWS, :] for s in range(16)], axis=0)
    row = lax.broadcasted_iota(jnp.int32, (64, 256), 0)
    col = lax.broadcasted_iota(jnp.int32, (64, 256), 1)
    pick = jnp.zeros((64, 256), jnp.bool_)
    for s, (distance, other) in enumerate(DISTANCE):
        owner_core = core if other == 0 else 1 - core
        owner = ((z + distance + NZ) % NZ) * 4 + y * 2 + owner_core
        pick = pick | (((row % 32) == owner) & (col == 16 * s + row // 32))
    by_depth = lax.dot_general(
        jnp.where(pick, 1.0, 0.0).astype(BF), label_rows, NN, preferred_element_type=F32
    )

    def at_depth(depth):
        chosen = jnp.sum(jnp.where(col == depth, by_depth, 0.0), axis=1, keepdims=True)
        return jnp.broadcast_to(chosen, (64, 128))

    lab_send[...] = at_depth(tok + 2 - 4 * y)
    o_copy = send(o_send, o_recv, y_send.at[1], y_recv.at[1], across)
    lse_copy = send(lse_send, lse_recv, y_send.at[2], y_recv.at[2], across)
    lab_copy = send(lab_send, lab_recv, y_send.at[3], y_recv.at[3], across)
    attend(0, TILES[3])
    attend(0, TILES[4])
    own_part, my_lse = finish(0)
    lse_copy.wait_recv()
    head0 = jnp.broadcast_to(lse_recv[0:1], (64, TOK))
    head1 = jnp.broadcast_to(lse_recv[8:9], (64, TOK))
    its_lse = jnp.concatenate([head0, head1], axis=0).T
    top = jnp.maximum(my_lse, its_lse)
    my_share, its_share = jnp.exp2(my_lse - top), jnp.exp2(its_lse - top)
    both = my_share + its_share
    o_copy.wait_recv()
    merged = (my_share * own_part + its_share * o_recv[...].astype(F32)) / both
    attended[...] = merged.astype(BF)

    own = pltpu.make_async_copy(attended.at[own_rows], att_all.at[:, mine], local_sem.at[9])
    own.start()
    copies = []
    for i in range(7):
        theirs = lax.rem(heads + i + 1, 8)
        copies.append(
            send(
                attended.at[pl.ds(pl.multiple_of(theirs * 64, 64), 64)],
                att_all.at[:, mine],
                a_send.at[i],
                a_recv.at[i],
                others[i],
            )
        )
    lab_copy.wait_recv()
    labels = at_depth(tok) + lab_recv[...]

    def start_halo(stage, halo):
        halves = []
        for i, (dh, dt) in enumerate(NEAR):
            src, dst = {0: ((32, 96), (32, 96)), 1: ((64, 96), (0, 32)), -1: ((32, 64), (96, 128))}[dh]
            halves.append(
                send(
                    halo.at[1, src[0] : src[1]],
                    halo.at[1 - dt, dst[0] : dst[1]],
                    h_send.at[stage, i],
                    h_recv.at[stage, i],
                    near[i],
                )
            )
        return halves

    def end_halo(halo, halves):
        width = halo.shape[2]
        for copy in halves:
            copy.wait_recv()

        @pl.when(heads == 0)
        def _():
            halo[:, 0:32] = jnp.zeros((3, 32, width), BF)

        @pl.when(heads == 7)
        def _():
            halo[:, 96:128] = jnp.zeros((3, 32, width), BF)

        @pl.when(tok == 0)
        def _():
            halo[0] = jnp.zeros((128, width), BF)

        @pl.when(tok == 31)
        def _():
            halo[2] = jnp.zeros((128, width), BF)

    def conv(halo, weights, flipped):
        groups = halo.shape[2] // 256
        parts = []
        for e in range(3):
            total = None
            for a in range(3):
                for b in range(3):
                    c, t = (2 - a, 2 - b) if flipped else (a, b)
                    window = [halo[t, 32 * c : 32 * c + 64, 256 * g : 256 * g + 256] for g in range(groups)]
                    term = lax.dot_general(
                        jnp.concatenate(window, axis=0),
                        weights[(a * 3 + b) * 3 + e],
                        NT if flipped else NN,
                        preferred_element_type=F32,
                    )
                    total = term if total is None else total + term
            parts.append(total)
        if flipped:
            parts = parts[::-1]
        rows = 64 * groups
        inline = lax.broadcasted_iota(jnp.int32, (rows, 256), 0) % 32
        before = jnp.where(inline == 0, 0.0, pltpu.roll(parts[0], 1, 0))
        after = jnp.where(inline == 31, 0.0, pltpu.roll(parts[2], rows - 1, 0))
        return before + parts[1] + after

    def sigmoid(v):
        return 1.0 / (1.0 + jnp.exp(-v))

    for load in loads:
        load.wait()
    for copy in w_copies:
        copy.wait_recv()
    own.wait()
    for copy in copies:
        copy.wait_recv()
    projected = lax.dot_general(att_all[...], wf[...], NN, preferred_element_type=F32)
    encoded = (residual[...].astype(F32) + projected).astype(BF)
    halo_one[1, 32:96] = lax.dot_general(encoded, neck[...], NN, preferred_element_type=F32).astype(BF)
    halves = start_halo(0, halo_one)
    result[0] = encoded
    enc_copy = pltpu.make_async_copy(result.at[0], enc_hbm, local_sem.at[10])
    enc_copy.start()
    end_halo(halo_one, halves)
    hidden_one = conv(halo_one, first, False)
    gate_one = sigmoid(hidden_one)
    halo_two[1, 32:96] = (hidden_one * gate_one).astype(BF)
    halves = start_halo(1, halo_two)
    slope_one = gate_one * (1.0 + hidden_one * (1.0 - gate_one))
    end_halo(halo_two, halves)
    hidden_two = conv(halo_two, second, False)
    gate_two = sigmoid(hidden_two)
    active_two = (hidden_two * gate_two).astype(BF).astype(F32)
    w_class = w_class_buf[...].astype(F32)
    logits = jnp.sum(active_two * w_class, axis=1, keepdims=True)
    probability = jnp.broadcast_to(sigmoid(logits), (64, 128))
    spread = probability * (1.0 - probability)
    slope_two = gate_two * (1.0 + hidden_two * (1.0 - gate_two))
    unscaled = jnp.concatenate([spread, spread], axis=1) * w_class * slope_two
    halo_three[1, 32:96, 0:256] = unscaled.astype(BF)
    halo_three[1, 32:96, 256:384] = labels.astype(BF)
    halves = start_halo(2, halo_three)

    def over_cells(value):
        return jnp.sum(value, axis=0, keepdims=True)

    row8 = lax.broadcasted_iota(jnp.int32, (8, 128), 0)
    stats = jnp.where(
        row8 == 0,
        over_cells(probability * labels),
        jnp.where(row8 == 1, over_cells(probability), over_cells(labels)),
    )
    index_a = heads * 2 + core
    send_a[...] = stats
    stat_copies = [
        send(send_a, stat_a.at[index_a], s_send.at[d], s_recv.at[d], group_a[d]) for d in range(15)
    ]
    stat_a[index_a] = stats
    end_halo(halo_three, halves)
    for copy in stat_copies:
        copy.wait_recv()
    partial = stat_a[0]
    for i in range(1, 16):
        partial = partial + stat_a[i]
    index_b = z * 2 + y
    send_b[...] = partial
    stat_copies = [
        send(send_b, stat_b.at[index_b], r_send.at[d], r_recv.at[d], group_b[d]) for d in range(15)
    ]
    stat_b[index_b] = partial
    for t in range(3):
        cells = halo_three[t, :, 256:384]
        cells = jnp.concatenate([cells, cells], axis=1).astype(F32)
        slopes = halo_three[t, :, 0:256].astype(F32)
        grad_two[t, :, 0:256] = (slopes * cells).astype(BF)
        grad_two[t, :, 256:512] = (slopes * (1.0 - cells)).astype(BF)
    grad_active = conv(grad_two, second, True)
    halo_four[1, 32:96, 0:256] = (grad_active[0:64] * slope_one).astype(BF)
    halo_four[1, 32:96, 256:512] = (grad_active[64:128] * slope_one).astype(BF)
    halves = start_halo(3, halo_four)
    end_halo(halo_four, halves)
    by_kind = conv(halo_four, first, True)
    for copy in stat_copies:
        copy.wait_recv()
    sums = stat_b[0]
    for i in range(1, 16):
        sums = sums + stat_b[i]
    intersection, denominator = sums[0:1], sums[1:2] + sums[2:3]
    loss_ref[0, 0] = (1.0 - 2.0 * intersection / denominator)[0, 0]
    scale = LOSS_SCALE * 16384.0 * -2.0 / (denominator * denominator)
    fault, rest = scale * (denominator - intersection), scale * -intersection
    fault, rest = jnp.concatenate([fault, fault], axis=1), jnp.concatenate([rest, rest], axis=1)
    grad_neck = (by_kind[0:64] * fault + by_kind[64:128] * rest).astype(BF)
    result[1] = lax.dot_general(grad_neck, neck[...], NT, preferred_element_type=F32).astype(BF)
    grad_copy = pltpu.make_async_copy(result.at[1], grad_hbm, local_sem.at[11])
    grad_copy.start()
    enc_copy.wait()
    for copy in sent:
        copy.wait_send()
    grad_copy.wait()


def block(queries, key_rows, value_rows, labels, w_out, residual, w_neck, w_first, w_second, w_class):
    dma = pltpu.SemaphoreType.DMA
    vmem, anywhere = pl.BlockSpec(memory_space=pltpu.VMEM), pl.BlockSpec(memory_space=pl.ANY)
    return pl.pallas_call(
        block_kernel,
        out_shape=(
            jax.ShapeDtypeStruct((64, 1024), BF),
            jax.ShapeDtypeStruct((1, 1), F32),
            jax.ShapeDtypeStruct((64, 1024), BF),
        ),
        in_specs=[anywhere] * 3 + [vmem] + [anywhere] * 6,
        out_specs=(anywhere, pl.BlockSpec(memory_space=pltpu.SMEM), anywhere),
        scratch_shapes=[
            pltpu.VMEM((16, ROWS, 256), BF),
            pltpu.VMEM((2, TOK, 128), BF),
            pltpu.VMEM((2, 2 * TOK, 256), BF),
            pltpu.VMEM((2 * TOK, 256), F32),
            pltpu.VMEM((2, 2 * TOK, 128), F32),
            pltpu.VMEM((TOK, 128), BF),
            pltpu.VMEM((TOK, 128), BF),
            pltpu.VMEM((16, TOK), F32),
            pltpu.VMEM((16, TOK), F32),
            pltpu.VMEM((64, 128), F32),
            pltpu.VMEM((64, 128), F32),
            pltpu.VMEM((TOK, 128), BF),
            pltpu.VMEM((64, 1024), BF),
            pltpu.VMEM((1024, 1024), BF),
            pltpu.VMEM((1024, 256), BF),
            pltpu.VMEM((27, 256, 256), BF),
            pltpu.VMEM((27, 256, 256), BF),
            pltpu.VMEM((64, 1024), BF),
            pltpu.VMEM((1, 256), BF),
            pltpu.VMEM((2, 64, 1024), BF),
            pltpu.VMEM((3, 128, 256), BF),
            pltpu.VMEM((3, 128, 256), BF),
            pltpu.VMEM((3, 128, 384), BF),
            pltpu.VMEM((3, 128, 512), BF),
            pltpu.VMEM((3, 128, 512), BF),
            pltpu.VMEM((16, 8, 128), F32),
            pltpu.VMEM((16, 8, 128), F32),
            pltpu.VMEM((8, 128), F32),
            pltpu.VMEM((8, 128), F32),
            dma((12,)),
            dma((16,)),
            dma((32,)),
            dma((32,)),
            dma((4,)),
            dma((4,)),
            dma((7,)),
            dma((7,)),
            dma((7,)),
            dma((7,)),
            dma((4, 8)),
            dma((4, 8)),
            dma((15,)),
            dma((15,)),
            dma((15,)),
            dma((15,)),
        ],
        compiler_params=pltpu.CompilerParams(
            collective_id=0, has_side_effects=True, vmem_limit_bytes=67043328
        ),
        name="block",
    )(queries, key_rows, value_rows, labels, w_out, residual, w_neck, w_first, w_second, w_class)


def on_device(
    queries, key_rows, value_rows, residual, w_out, w_neck, w_first, w_second, w_class, labels
):
    encoded, loss, grad = block(
        queries.reshape(TOK, 128),
        key_rows.reshape(TOK, 128),
        value_rows.reshape(TOK, 128),
        labels.reshape(2, 32),
        w_out,
        residual.reshape(64, 1024),
        w_neck,
        w_first.reshape(27, 256, 256),
        w_second.reshape(27, 256, 256),
        w_class.reshape(1, 256),
    )
    shape = residual.shape
    return (encoded.reshape(shape), loss.reshape(()), grad.reshape(shape))


def solution(mesh):
    slab = P("tok", None, None, "heads")
    rows = P("heads", "tok", None, None)
    placed = (slab, slab, slab, rows, P("heads", None), P(), P(), P(), P(), P("heads", None, "tok"))
    return jax.shard_map(
        on_device, mesh=mesh, in_specs=placed, out_specs=(rows, P(), rows), check_vma=False
    )
```

time: 108 us -> 92 us (0.85)
  Pallas kernels: 94.3 us -> 85.1 us
  local copies, waits for them, and re-layouts: 12.3 us -> 4.36 us
  between operations: 0.66 us -> 2.41 us
    pallas_call x2 -> x1, Pallas kernels: 94.3 us -> 85.1 us  [block(): pl.pallas_call(block_kernel, out_shape=(jax.ShapeDtypeStruct((64, 1024),...]
    unnamed x17 -> x2, local copies, waits for them, and re-layouts: 10.5 us -> 3.14 us
    reshape x0 -> x1, local copies, waits for them, and re-layouts: none -> 1.22 us  [on_device(): w_class.reshape(1, 256)]
where the time goes in v2:
time: 92 us; the launch traced here: 91.8 us
  Pallas kernels  85.1 us (92%)
  local copies, waits for them, and re-layouts  4.36 us (5%)
  between operations  2.41 us (3%)
    pallas_call x1, Pallas kernels, block(): pl.pallas_call(block_kernel, out_shape=(jax.ShapeDtypeStruct((64, 1024),...  85.1 us
    unnamed x2, local copies, waits for them, and re-layouts  3.14 us

profile of v2, /device:TPU:1, one launch (start us, length us, event | category | flops | bytes accessed | tf_op | source)
XLA Modules:
  0.0 91.8 jit_solution(15001443941739312017)
XLA Ops:
  0.6 1.2 %reshape.46.class_hbm = bf16[1,256]{1,0:T(2,128)(2,1)} reshape(bf16[256]{0:T(256)(128)(2,1)} %param.18) | data formatting | bytes 1024 | tf_op jit(solution)/shard_map/reshape | solution.py:522
  1.9 85.1 %block.1 = (bf16[64,1024]{1,0:T(8,128)(2,1)}, f32[1,1]{1,0:T(1,128)}, bf16[64,1024]{1,0:T(8,128)(2,1)}) custom-call(bf16[512,128]{1,0:T(8,128)(2,1)} %bitcast.16, bf16[512,128]{1,0:T(8,128)(2,1)} %bitcast.17, bf16[512,128]{1,0:T(8,128)(2,1)} %bitcast.18, s32[2,32]{1,0:T(2,128)} %bitcast.22, bf16[128,1024]{1,0:T(8,128)(2,1)} %w_hbm.1, ...), custom_call_target="tpu_custom_call" | custom-call | tf_op jit(solution)/shard_map/block/pallas_call | solution.py:446
  86.9 1.6 %copy.18 = bf16[2,1,32,1024]{3,2,1,0:T(8,128)(2,1)} copy(bf16[2,1,32,1024]{3,2,1,0:T(8,128)(2,1)} %bitcast.21) | data formatting | bytes 262144
  89.1 1.6 %copy.20 = bf16[2,1,32,1024]{3,2,1,0:T(8,128)(2,1)} copy(bf16[2,1,32,1024]{3,2,1,0:T(8,128)(2,1)} %bitcast.20) | data formatting | bytes 262144

commit v3 on v2

--- a/solution.py
+++ b/solution.py
@@ -36,15 +36,16 @@
     return {"heads": heads, "tok": tok}
 
 
-NEAR = [(dh, dt) for dh in (-1, 0, 1) for dt in (-1, 0, 1) if (dh, dt) != (0, 0)]
+FAR, OWN, MATE = 0, 1, 2
+NEAR = [(0, FAR), (1, FAR), (-1, FAR), (1, OWN), (-1, OWN), (1, MATE), (-1, MATE), (0, MATE)]
 PARTS = ((0, TOK // 2), (TOK // 2, ROWS))
 
 
 def block_kernel(
-    q_hbm, k_hbm, v_hbm, lab_ref, w_hbm, res_hbm, neck_hbm, first_hbm, second_hbm, class_hbm,
+    q_hbm, k_hbm, v_hbm, lab_ref, w_hbm, res_hbm, neck_hbm, first_hbm, second_hbm, class_ref,
     enc_hbm, loss_ref, grad_hbm,
     kv, q_buf, qx, acc, peak, o_send, o_recv, lse_send, lse_recv, lab_send, lab_recv, attended,
-    att_all, wf, neck, first, second, residual, w_class_buf, result,
+    att_all, wf, neck, first, second, residual, result,
     halo_one, halo_two, halo_three, halo_four, grad_two, stat_a, stat_b, send_a, send_b,
     local_sem, kv_send, kv_recv, mate_send, y_send, y_recv, w_send, w_recv,
     a_send, a_recv, h_send, h_recv, s_send, s_recv, r_send, r_recv,
@@ -55,7 +56,8 @@
     mate = at(heads, tok + 1 - 2 * core)
     across = at(heads, tok + 2 - 4 * y)
     others = [at((heads + d) % 8, tok) for d in range(1, 8)]
-    near = [at((heads + dh + 8) % 8, (tok + dt + 32) % 32) for dh, dt in NEAR]
+    beside = {FAR: (tok + 31 + 2 * core) % 32, OWN: tok, MATE: tok + 1 - 2 * core}
+    near = [at((heads + dh + 8) % 8, beside[plane]) for dh, plane in NEAR]
     group_a = [
         at((heads + d // 2) % 8, tok if d % 2 == 0 else tok + 1 - 2 * core) for d in range(1, 16)
     ]
@@ -80,7 +82,6 @@
                 (first_hbm, first),
                 (second_hbm, second),
                 (res_hbm, residual),
-                (class_hbm, w_class_buf),
             )
         )
     ]
@@ -95,9 +96,6 @@
     )
     lab_rows = jnp.concatenate([lab_rows, jnp.zeros((14, 256), F32)], axis=0)
     kv[0, TOK:ROWS, :] = lab_rows.astype(BF)
-    pl.semaphore_wait(barrier, len(peers))
-    for copy in local:
-        copy.wait()
 
     sent = []
 
@@ -193,15 +191,18 @@
         top = jnp.where(lane < HD, peak[0, rows], peak[1, rows])
         return acc[rows, 0:128] / total, top + jnp.log(total) * LOG2E
 
+    for copy in local:
+        copy.wait()
+    prepare(0)
+    pl.semaphore_wait(barrier, len(peers))
     q_copy = send(q_buf.at[0], q_buf.at[1], y_send.at[0], y_recv.at[0], across)
     for part in range(2):
         ring(0, part)
     for part in range(2):
         share(0, part)
-    prepare(0)
+    w_copies = [send(wf.at[mine], wf.at[mine], w_send.at[d], w_recv.at[d], others[d]) for d in (3, 2, 4, 1, 5, 0, 6)]
     await_mate(0)
     attend(0, TILES[0])
-    w_copies = [send(wf.at[mine], wf.at[mine], w_send.at[d], w_recv.at[d], others[d]) for d in range(7)]
     for load in loads:
         load.start()
     q_copy.wait_recv()
@@ -230,8 +231,8 @@
     part, lse = finish(1)
     o_send[...] = part.astype(BF)
     flat = lse.T
-    lse_send[0:8] = flat[0:8]
-    lse_send[8:16] = flat[64:72]
+    row8 = lax.broadcasted_iota(jnp.int32, (8, TOK), 0)
+    lse_send[...] = jnp.where(row8 < 4, jnp.broadcast_to(flat[0:1], (8, TOK)), jnp.broadcast_to(flat[64:65], (8, TOK)))
     label_rows = jnp.concatenate([kv[s, TOK:ROWS, :] for s in range(16)], axis=0)
     row = lax.broadcasted_iota(jnp.int32, (64, 256), 0)
     col = lax.broadcasted_iota(jnp.int32, (64, 256), 1)
@@ -248,7 +249,7 @@
         chosen = jnp.sum(jnp.where(col == depth, by_depth, 0.0), axis=1, keepdims=True)
         return jnp.broadcast_to(chosen, (64, 128))
 
-    lab_send[...] = at_depth(tok + 2 - 4 * y)
+    lab_send[...] = at_depth(tok + 2 - 4 * y).astype(BF)
     o_copy = send(o_send, o_recv, y_send.at[1], y_recv.at[1], across)
     lse_copy = send(lse_send, lse_recv, y_send.at[2], y_recv.at[2], across)
     lab_copy = send(lab_send, lab_recv, y_send.at[3], y_recv.at[3], across)
@@ -257,7 +258,7 @@
     own_part, my_lse = finish(0)
     lse_copy.wait_recv()
     head0 = jnp.broadcast_to(lse_recv[0:1], (64, TOK))
-    head1 = jnp.broadcast_to(lse_recv[8:9], (64, TOK))
+    head1 = jnp.broadcast_to(lse_recv[4:5], (64, TOK))
     its_lse = jnp.concatenate([head0, head1], axis=0).T
     top = jnp.maximum(my_lse, its_lse)
     my_share, its_share = jnp.exp2(my_lse - top), jnp.exp2(its_lse - top)
@@ -281,16 +282,16 @@
             )
         )
     lab_copy.wait_recv()
-    labels = at_depth(tok) + lab_recv[...]
+    labels = at_depth(tok) + lab_recv[...].astype(F32)
 
     def start_halo(stage, halo):
         halves = []
-        for i, (dh, dt) in enumerate(NEAR):
+        for i, (dh, plane) in enumerate(NEAR):
             src, dst = {0: ((32, 96), (32, 96)), 1: ((64, 96), (0, 32)), -1: ((32, 64), (96, 128))}[dh]
             halves.append(
                 send(
-                    halo.at[1, src[0] : src[1]],
-                    halo.at[1 - dt, dst[0] : dst[1]],
+                    halo.at[OWN, src[0] : src[1]],
+                    halo.at[plane, dst[0] : dst[1]],
                     h_send.at[stage, i],
                     h_recv.at[stage, i],
                     near[i],
@@ -298,44 +299,42 @@
             )
         return halves
 
-    def end_halo(halo, halves):
+    def end_plane(halo, halves, plane):
         width = halo.shape[2]
-        for copy in halves:
-            copy.wait_recv()
+        for copy, (_, its_plane) in zip(halves, NEAR):
+            if its_plane == plane:
+                copy.wait_recv()
 
         @pl.when(heads == 0)
         def _():
-            halo[:, 0:32] = jnp.zeros((3, 32, width), BF)
+            halo[plane, 0:32] = jnp.zeros((32, width), BF)
 
         @pl.when(heads == 7)
         def _():
-            halo[:, 96:128] = jnp.zeros((3, 32, width), BF)
-
-        @pl.when(tok == 0)
-        def _():
-            halo[0] = jnp.zeros((128, width), BF)
-
-        @pl.when(tok == 31)
-        def _():
-            halo[2] = jnp.zeros((128, width), BF)
-
-    def conv(halo, weights, flipped):
+            halo[plane, 96:128] = jnp.zeros((32, width), BF)
+
+        if plane == FAR:
+
+            @pl.when((tok == 0) | (tok == 31))
+            def _():
+                halo[plane] = jnp.zeros((128, width), BF)
+
+    def conv(halo, ready, weights, flipped):
         groups = halo.shape[2] // 256
-        parts = []
-        for e in range(3):
-            total = None
+        parts = [None] * 3
+        for plane in (OWN, MATE, FAR):
+            ready(plane)
+            away = {OWN: 1, MATE: 2 - 2 * core, FAR: 2 * core}[plane]
+            b = 2 - away if flipped else away
             for a in range(3):
-                for b in range(3):
-                    c, t = (2 - a, 2 - b) if flipped else (a, b)
-                    window = [halo[t, 32 * c : 32 * c + 64, 256 * g : 256 * g + 256] for g in range(groups)]
+                c = 2 - a if flipped else a
+                window = [halo[plane, 32 * c : 32 * c + 64, 256 * g : 256 * g + 256] for g in range(groups)]
+                window = jnp.concatenate(window, axis=0)
+                for e in range(3):
                     term = lax.dot_general(
-                        jnp.concatenate(window, axis=0),
-                        weights[(a * 3 + b) * 3 + e],
-                        NT if flipped else NN,
-                        preferred_element_type=F32,
+                        window, weights[(a * 3 + b) * 3 + e], NT if flipped else NN, preferred_element_type=F32
                     )
-                    total = term if total is None else total + term
-            parts.append(total)
+                    parts[e] = term if parts[e] is None else parts[e] + term
         if flipped:
             parts = parts[::-1]
         rows = 64 * groups
@@ -357,21 +356,19 @@
     projected = lax.dot_general(att_all[...], wf[...], NN, preferred_element_type=F32)
     encoded = (residual[...].astype(F32) + projected).astype(BF)
     halo_one[1, 32:96] = lax.dot_general(encoded, neck[...], NN, preferred_element_type=F32).astype(BF)
-    halves = start_halo(0, halo_one)
+    halves_one = start_halo(0, halo_one)
     result[0] = encoded
     enc_copy = pltpu.make_async_copy(result.at[0], enc_hbm, local_sem.at[10])
     enc_copy.start()
-    end_halo(halo_one, halves)
-    hidden_one = conv(halo_one, first, False)
+    hidden_one = conv(halo_one, lambda plane: end_plane(halo_one, halves_one, plane), first, False)
     gate_one = sigmoid(hidden_one)
     halo_two[1, 32:96] = (hidden_one * gate_one).astype(BF)
-    halves = start_halo(1, halo_two)
+    halves_two = start_halo(1, halo_two)
     slope_one = gate_one * (1.0 + hidden_one * (1.0 - gate_one))
-    end_halo(halo_two, halves)
-    hidden_two = conv(halo_two, second, False)
+    hidden_two = conv(halo_two, lambda plane: end_plane(halo_two, halves_two, plane), second, False)
     gate_two = sigmoid(hidden_two)
     active_two = (hidden_two * gate_two).astype(BF).astype(F32)
-    w_class = w_class_buf[...].astype(F32)
+    w_class = class_ref[...].reshape(1, 256).astype(F32)
     logits = jnp.sum(active_two * w_class, axis=1, keepdims=True)
     probability = jnp.broadcast_to(sigmoid(logits), (64, 128))
     spread = probability * (1.0 - probability)
@@ -379,7 +376,7 @@
     unscaled = jnp.concatenate([spread, spread], axis=1) * w_class * slope_two
     halo_three[1, 32:96, 0:256] = unscaled.astype(BF)
     halo_three[1, 32:96, 256:384] = labels.astype(BF)
-    halves = start_halo(2, halo_three)
+    halves_three = start_halo(2, halo_three)
 
     def over_cells(value):
         return jnp.sum(value, axis=0, keepdims=True)
@@ -396,31 +393,32 @@
         send(send_a, stat_a.at[index_a], s_send.at[d], s_recv.at[d], group_a[d]) for d in range(15)
     ]
     stat_a[index_a] = stats
-    end_halo(halo_three, halves)
+    index_b = z * 2 + y
+
+    def split_kinds(plane):
+        end_plane(halo_three, halves_three, plane)
+        cells = halo_three[plane, :, 256:384]
+        cells = jnp.concatenate([cells, cells], axis=1).astype(F32)
+        slopes = halo_three[plane, :, 0:256].astype(F32)
+        grad_two[plane, :, 0:256] = (slopes * cells).astype(BF)
+        grad_two[plane, :, 256:512] = (slopes * (1.0 - cells)).astype(BF)
+
+    grad_active = conv(grad_two, split_kinds, second, True)
+    halo_four[1, 32:96, 0:256] = (grad_active[0:64] * slope_one).astype(BF)
+    halo_four[1, 32:96, 256:512] = (grad_active[64:128] * slope_one).astype(BF)
+    halves_four = start_halo(3, halo_four)
     for copy in stat_copies:
         copy.wait_recv()
     partial = stat_a[0]
     for i in range(1, 16):
         partial = partial + stat_a[i]
-    index_b = z * 2 + y
     send_b[...] = partial
-    stat_copies = [
+    total_copies = [
         send(send_b, stat_b.at[index_b], r_send.at[d], r_recv.at[d], group_b[d]) for d in range(15)
     ]
     stat_b[index_b] = partial
-    for t in range(3):
-        cells = halo_three[t, :, 256:384]
-        cells = jnp.concatenate([cells, cells], axis=1).astype(F32)
-        slopes = halo_three[t, :, 0:256].astype(F32)
-        grad_two[t, :, 0:256] = (slopes * cells).astype(BF)
-        grad_two[t, :, 256:512] = (slopes * (1.0 - cells)).astype(BF)
-    grad_active = conv(grad_two, second, True)
-    halo_four[1, 32:96, 0:256] = (grad_active[0:64] * slope_one).astype(BF)
-    halo_four[1, 32:96, 256:512] = (grad_active[64:128] * slope_one).astype(BF)
-    halves = start_halo(3, halo_four)
-    end_halo(halo_four, halves)
-    by_kind = conv(halo_four, first, True)
-    for copy in stat_copies:
+    by_kind = conv(halo_four, lambda plane: end_plane(halo_four, halves_four, plane), first, True)
+    for copy in total_copies:
         copy.wait_recv()
     sums = stat_b[0]
     for i in range(1, 16):
@@ -450,7 +448,7 @@
             jax.ShapeDtypeStruct((1, 1), F32),
             jax.ShapeDtypeStruct((64, 1024), BF),
         ),
-        in_specs=[anywhere] * 3 + [vmem] + [anywhere] * 6,
+        in_specs=[anywhere] * 3 + [vmem] + [anywhere] * 5 + [vmem],
         out_specs=(anywhere, pl.BlockSpec(memory_space=pltpu.SMEM), anywhere),
         scratch_shapes=[
             pltpu.VMEM((16, ROWS, 256), BF),
@@ -460,10 +458,10 @@
             pltpu.VMEM((2, 2 * TOK, 128), F32),
             pltpu.VMEM((TOK, 128), BF),
             pltpu.VMEM((TOK, 128), BF),
-            pltpu.VMEM((16, TOK), F32),
-            pltpu.VMEM((16, TOK), F32),
-            pltpu.VMEM((64, 128), F32),
-            pltpu.VMEM((64, 128), F32),
+            pltpu.VMEM((8, TOK), F32),
+            pltpu.VMEM((8, TOK), F32),
+            pltpu.VMEM((64, 128), BF),
+            pltpu.VMEM((64, 128), BF),
             pltpu.VMEM((TOK, 128), BF),
             pltpu.VMEM((64, 1024), BF),
             pltpu.VMEM((1024, 1024), BF),
@@ -471,7 +469,6 @@
             pltpu.VMEM((27, 256, 256), BF),
             pltpu.VMEM((27, 256, 256), BF),
             pltpu.VMEM((64, 1024), BF),
-            pltpu.VMEM((1, 256), BF),
             pltpu.VMEM((2, 64, 1024), BF),
             pltpu.VMEM((3, 128, 256), BF),
             pltpu.VMEM((3, 128, 256), BF),
@@ -519,7 +516,7 @@
         w_neck,
         w_first.reshape(27, 256, 256),
         w_second.reshape(27, 256, 256),
-        w_class.reshape(1, 256),
+        w_class,
     )
     shape = residual.shape
     return (encoded.reshape(shape), loss.reshape(()), grad.reshape(shape))

time: 92 us -> 86.2 us (0.937)
  Pallas kernels: 85.1 us -> 80.5 us
  local copies, waits for them, and re-layouts: 4.36 us -> 3.14 us
    pallas_call x1, Pallas kernels: 85.1 us -> 80.5 us  [block(): pl.pallas_call(block_kernel, out_shape=(jax.ShapeDtypeStruct((64, 1024),...]
    reshape x1 -> x0, local copies, waits for them, and re-layouts: 1.22 us -> none  [on_device(): w_class.reshape(1, 256)]
where the time goes in v3:
time: 86.2 us; the launch traced here: 86.1 us
  Pallas kernels  80.5 us (93%)
  local copies, waits for them, and re-layouts  3.14 us (4%)
  between operations  2.41 us (3%)
    pallas_call x1, Pallas kernels, block(): pl.pallas_call(block_kernel, out_shape=(jax.ShapeDtypeStruct((64, 1024),...  80.5 us
    unnamed x2, local copies, waits for them, and re-layouts  3.14 us

profile of v3, /device:TPU:1, one launch (start us, length us, event | category | flops | bytes accessed | tf_op | source)
XLA Modules:
  0.0 86.1 jit_solution(8046506167955405759)
XLA Ops:
  0.6 80.5 %block.1 = (bf16[64,1024]{1,0:T(8,128)(2,1)}, f32[1,1]{1,0:T(1,128)}, bf16[64,1024]{1,0:T(8,128)(2,1)}) custom-call(bf16[512,128]{1,0:T(8,128)(2,1)} %bitcast.16, bf16[512,128]{1,0:T(8,128)(2,1)} %bitcast.17, bf16[512,128]{1,0:T(8,128)(2,1)} %bitcast.18, s32[2,32]{1,0:T(2,128)} %bitcast.22, bf16[128,1024]{1,0:T(8,128)(2,1)} %w_hbm.1, ...), custom_call_target="tpu_custom_call" | custom-call | tf_op jit(solution)/shard_map/block/pallas_call | solution.py:444
  81.2 1.6 %copy.18 = bf16[2,1,32,1024]{3,2,1,0:T(8,128)(2,1)} copy(bf16[2,1,32,1024]{3,2,1,0:T(8,128)(2,1)} %bitcast.21) | data formatting | bytes 262144
  83.4 1.6 %copy.20 = bf16[2,1,32,1024]{3,2,1,0:T(8,128)(2,1)} copy(bf16[2,1,32,1024]{3,2,1,0:T(8,128)(2,1)} %bitcast.20) | data formatting | bytes 262144

commit v4 on v3

--- a/solution.py
+++ b/solution.py
@@ -201,8 +201,9 @@
     for part in range(2):
         share(0, part)
     w_copies = [send(wf.at[mine], wf.at[mine], w_send.at[d], w_recv.at[d], others[d]) for d in (3, 2, 4, 1, 5, 0, 6)]
+    attend(0, (0,))
     await_mate(0)
-    attend(0, TILES[0])
+    attend(0, (1,))
     for load in loads:
         load.start()
     q_copy.wait_recv()
@@ -210,21 +211,22 @@
     arrive(1, 0)
     attend(1, TILES[0])
     arrive(1, 1)
+    attend(0, TILES[1][0:2])
     await_mate(-1, 1)
-    attend(0, TILES[1])
+    attend(0, TILES[1][2:4])
     arrive(2, 0)
+    arrive(2, 1)
     attend(1, TILES[1])
-    arrive(2, 1)
     await_mate(-2, 2)
     attend(0, TILES[2])
     arrive(3, 0)
+    arrive(3, 1)
     attend(1, TILES[2])
-    arrive(3, 1)
     await_mate(-3, 3)
-    attend(1, TILES[3])
     for part in range(2):
         arrivals[(4, 0, part)].wait_recv()
         share(4, part)
+    attend(1, TILES[3])
     await_mate(4)
     attend(1, TILES[4])
 

time: 86.2 us -> 84.2 us (0.977)
  Pallas kernels: 80.5 us -> 78.5 us
    pallas_call x1, Pallas kernels: 80.5 us -> 78.5 us  [block(): pl.pallas_call(block_kernel, out_shape=(jax.ShapeDtypeStruct((64, 1024),...]
where the time goes in v4:
time: 84.2 us; the launch traced here: 84.1 us
  Pallas kernels  78.5 us (93%)
  local copies, waits for them, and re-layouts  3.14 us (4%)
  between operations  2.41 us (3%)
    pallas_call x1, Pallas kernels, block(): pl.pallas_call(block_kernel, out_shape=(jax.ShapeDtypeStruct((64, 1024),...  78.5 us
    unnamed x2, local copies, waits for them, and re-layouts  3.14 us

profile of v4, /device:TPU:1, one launch (start us, length us, event | category | flops | bytes accessed | tf_op | source)
XLA Modules:
  0.0 84.1 jit_solution(8007788104698173123)
XLA Ops:
  0.6 78.5 %block.1 = (bf16[64,1024]{1,0:T(8,128)(2,1)}, f32[1,1]{1,0:T(1,128)}, bf16[64,1024]{1,0:T(8,128)(2,1)}) custom-call(bf16[512,128]{1,0:T(8,128)(2,1)} %bitcast.16, bf16[512,128]{1,0:T(8,128)(2,1)} %bitcast.17, bf16[512,128]{1,0:T(8,128)(2,1)} %bitcast.18, s32[2,32]{1,0:T(2,128)} %bitcast.22, bf16[128,1024]{1,0:T(8,128)(2,1)} %w_hbm.1, ...), custom_call_target="tpu_custom_call" | custom-call | tf_op jit(solution)/shard_map/block/pallas_call | solution.py:446
  79.1 1.6 %copy.18 = bf16[2,1,32,1024]{3,2,1,0:T(8,128)(2,1)} copy(bf16[2,1,32,1024]{3,2,1,0:T(8,128)(2,1)} %bitcast.21) | data formatting | bytes 262144
  81.4 1.6 %copy.20 = bf16[2,1,32,1024]{3,2,1,0:T(8,128)(2,1)} copy(bf16[2,1,32,1024]{3,2,1,0:T(8,128)(2,1)} %bitcast.20) | data formatting | bytes 262144

commit v5 on v4

--- a/solution.py
+++ b/solution.py
@@ -43,9 +43,9 @@
 
 def block_kernel(
     q_hbm, k_hbm, v_hbm, lab_ref, w_hbm, res_hbm, neck_hbm, first_hbm, second_hbm, class_ref,
-    enc_hbm, loss_ref, grad_hbm,
+    enc_ref, loss_ref, grad_ref,
     kv, q_buf, qx, acc, peak, o_send, o_recv, lse_send, lse_recv, lab_send, lab_recv, attended,
-    att_all, wf, neck, first, second, residual, result,
+    att_all, wf, neck, first, second, residual,
     halo_one, halo_two, halo_three, halo_four, grad_two, stat_a, stat_b, send_a, send_b,
     local_sem, kv_send, kv_recv, mate_send, y_send, y_recv, w_send, w_recv,
     a_send, a_recv, h_send, h_recv, s_send, s_recv, r_send, r_recv,
@@ -359,9 +359,7 @@
     encoded = (residual[...].astype(F32) + projected).astype(BF)
     halo_one[1, 32:96] = lax.dot_general(encoded, neck[...], NN, preferred_element_type=F32).astype(BF)
     halves_one = start_halo(0, halo_one)
-    result[0] = encoded
-    enc_copy = pltpu.make_async_copy(result.at[0], enc_hbm, local_sem.at[10])
-    enc_copy.start()
+    enc_ref[...] = encoded
     hidden_one = conv(halo_one, lambda plane: end_plane(halo_one, halves_one, plane), first, False)
     gate_one = sigmoid(hidden_one)
     halo_two[1, 32:96] = (hidden_one * gate_one).astype(BF)
@@ -431,13 +429,9 @@
     fault, rest = scale * (denominator - intersection), scale * -intersection
     fault, rest = jnp.concatenate([fault, fault], axis=1), jnp.concatenate([rest, rest], axis=1)
     grad_neck = (by_kind[0:64] * fault + by_kind[64:128] * rest).astype(BF)
-    result[1] = lax.dot_general(grad_neck, neck[...], NT, preferred_element_type=F32).astype(BF)
-    grad_copy = pltpu.make_async_copy(result.at[1], grad_hbm, local_sem.at[11])
-    grad_copy.start()
-    enc_copy.wait()
+    grad_ref[...] = lax.dot_general(grad_neck, neck[...], NT, preferred_element_type=F32).astype(BF)
     for copy in sent:
         copy.wait_send()
-    grad_copy.wait()
 
 
 def block(queries, key_rows, value_rows, labels, w_out, residual, w_neck, w_first, w_second, w_class):
@@ -451,7 +445,7 @@
             jax.ShapeDtypeStruct((64, 1024), BF),
         ),
         in_specs=[anywhere] * 3 + [vmem] + [anywhere] * 5 + [vmem],
-        out_specs=(anywhere, pl.BlockSpec(memory_space=pltpu.SMEM), anywhere),
+        out_specs=(vmem, pl.BlockSpec(memory_space=pltpu.SMEM), vmem),
         scratch_shapes=[
             pltpu.VMEM((16, ROWS, 256), BF),
             pltpu.VMEM((2, TOK, 128), BF),
@@ -471,7 +465,6 @@
             pltpu.VMEM((27, 256, 256), BF),
             pltpu.VMEM((27, 256, 256), BF),
             pltpu.VMEM((64, 1024), BF),
-            pltpu.VMEM((2, 64, 1024), BF),
             pltpu.VMEM((3, 128, 256), BF),
             pltpu.VMEM((3, 128, 256), BF),
             pltpu.VMEM((3, 128, 384), BF),
@@ -481,7 +474,7 @@
             pltpu.VMEM((16, 8, 128), F32),
             pltpu.VMEM((8, 128), F32),
             pltpu.VMEM((8, 128), F32),
-            dma((12,)),
+            dma((10,)),
             dma((16,)),
             dma((32,)),
             dma((32,)),
@@ -499,7 +492,7 @@
             dma((15,)),
         ],
         compiler_params=pltpu.CompilerParams(
-            collective_id=0, has_side_effects=True, vmem_limit_bytes=67043328
+            collective_id=0, has_side_effects=True, vmem_limit_bytes=48 << 20
         ),
         name="block",
     )(queries, key_rows, value_rows, labels, w_out, residual, w_neck, w_first, w_second, w_class)
@@ -508,7 +501,7 @@
 def on_device(
     queries, key_rows, value_rows, residual, w_out, w_neck, w_first, w_second, w_class, labels
 ):
-    encoded, loss, grad = block(
+    operands = (
         queries.reshape(TOK, 128),
         key_rows.reshape(TOK, 128),
         value_rows.reshape(TOK, 128),
@@ -520,6 +513,7 @@
         w_second.reshape(27, 256, 256),
         w_class,
     )
+    encoded, loss, grad = block(*(pltpu.with_memory_space_constraint(operand, pltpu.HBM) for operand in operands))
     shape = residual.shape
     return (encoded.reshape(shape), loss.reshape(()), grad.reshape(shape))
 

time: 84.2 us -> 81.8 us (0.971)
  local copies, waits for them, and re-layouts: 3.14 us -> 1.32 us
    unnamed x2, local copies, waits for them, and re-layouts: 3.14 us -> 1.32 us
where the time goes in v5:
time: 81.8 us; the launch traced here: 81.7 us
  Pallas kernels  78 us (95%)
  between operations  2.34 us (3%)
  local copies, waits for them, and re-layouts  1.32 us (2%)
    pallas_call x1, Pallas kernels, block(): pl.pallas_call(block_kernel, out_shape=(jax.ShapeDtypeStruct((64, 1024),...  78 us

profile of v5, /device:TPU:1, one launch (start us, length us, event | category | flops | bytes accessed | tf_op | source)
XLA Modules:
  0.0 81.7 jit_solution(15209957111276386887)
XLA Ops:
  0.6 78.0 %block.1 = (bf16[64,1024]{1,0:T(8,128)(2,1)S(1)}, f32[1,1]{1,0:T(1,128)}, bf16[64,1024]{1,0:T(8,128)(2,1)S(1)}) custom-call(bf16[512,128]{1,0:T(8,128)(2,1)} %bitcast.18, bf16[512,128]{1,0:T(8,128)(2,1)} %bitcast.19, bf16[512,128]{1,0:T(8,128)(2,1)} %bitcast.20, s32[2,32]{1,0:T(2,128)} %bitcast.22, bf16[128,1024]{1,0:T(8,128)(2,1)} %w_hbm.1, ...), custom_call_target="tpu_custom_call" | custom-call | tf_op jit(solution)/shard_map/block/pallas_call | solution.py:440
  78.7 0.7 copy.18
  79.9 0.7 copy.20
